TPU v7x, 256 devices: a whole 4x4x8 slice. The times are simulated.
256 devices in a mesh: grp: 4 (over x), seq: 16 (over z_hi, y, core), mdl: 4 (over z_lo).
Axes of the slice: x: 4, y: 4, z: 8 (z_hi: 2, z_lo: 4; z = z_hi * 4 + z_lo), core: 2. Of those that a mesh axis runs over, the one named last changes fastest.
Arguments:
- layer_input: bfloat16 [8192, 8192], P('seq', 'grp'), may hold values from -64 to 64
- attn_weight: bfloat16 [8192, 8, 1280], P(('grp', 'seq'), 'mdl'), may hold values from -0.0625 to 0.0625
- rate_weight: bfloat16 [8192, 64], P('grp', 'mdl'), may hold values from -0.15625 to 0.15625
- rate_bias: float32 [64], P(('mdl', 'grp')), may hold values from -8 to -3
- decay_rate: float32 [64], P(('mdl', 'grp')), may hold values from 1e-05 to 0.1
- skip_gain: float32 [64], P(('mdl', 'grp')), may hold values from 0.5 to 1.5
Outputs:
- teacher_heads: bfloat16 [8192, 8192], P('seq', ('mdl', 'grp'))
- student_heads: bfloat16 [8192, 8192], P('seq', ('mdl', 'grp'))
All inputs are finite; a program needn't handle non-finite values.
Results may differ from a plain program's by a relative error of at most 0.03.
Values may be sent and summed in bfloat16 or wider, within the bound.
A program may use at most 192 MiB of HBM per device.

v0:
```python
import math

import jax
import jax.numpy as jnp
from jax import lax
from jax.sharding import PartitionSpec as P

HEADS = 64
KV_HEADS = 8
HEAD_DIM = 128
STRETCH = 256


ROPE_BASE = 500000.0
FAR_BELOW = -1e30


def cut_along(x, dim, count):
    before, after = (x.shape[:dim], x.shape[dim + 1 :])
    return jnp.moveaxis(x.reshape(*before, count, -1, *after), dim, 0)


def summed_on_arrival(x, axis, dim):
    count = lax.axis_size(axis)
    tiles = lax.all_to_all(cut_along(x, dim, count), axis, 0, 0, tiled=True)
    return jnp.sum(tiles, axis=0)


def copy_for_each(x, axis):
    count = lax.axis_size(axis)
    return lax.all_to_all(jnp.broadcast_to(x[None], (count, *x.shape)), axis, 0, 0, tiled=True)


def of_everyone(x, axis):
    everything = copy_for_each(x, axis)
    return jnp.sum(everything, axis=0)


def sent_together(arrays, axis, dim, along):
    widths = [math.prod(a.shape[along:]) for a in arrays]
    both = jnp.concatenate(
        [a.reshape(*a.shape[:along], w) for a, w in zip(arrays, widths)], axis=along
    )
    out = lax.all_gather(both, axis, axis=dim, tiled=True)
    tiles = jnp.split(out, [sum(widths[:k]) for k in range(1, len(widths))], axis=along)
    return tuple((b.reshape(*out.shape[:along], *a.shape[along:]) for a, b in zip(arrays, tiles)))


def rope_angles(positions):
    half = HEAD_DIM // 2
    freq = ROPE_BASE ** (-2.0 * jnp.arange(half, dtype=jnp.float32) / HEAD_DIM)
    angle = positions.astype(jnp.float32)[:, None] * freq[None, :]
    return (jnp.cos(angle), jnp.sin(angle))


def rotate(vectors, cosine, sine):
    half = vectors.shape[-1] // 2
    first = vectors[..., :half]
    second = vectors[..., half:]
    cosine = cosine[:, None, :]
    sine = sine[:, None, :]
    return jnp.concatenate(
        [first * cosine - second * sine, second * cosine + first * sine], axis=-1
    )


def state_product(cterm, state):
    high = state.astype(jnp.bfloat16)
    low = (state - high.astype(jnp.float32)).astype(jnp.bfloat16)
    upper = jnp.einsum("thn,hnp->thp", cterm, high, preferred_element_type=jnp.float32)
    return upper + jnp.einsum("thn,hnp->thp", cterm, low, preferred_element_type=jnp.float32)


def key_absorber(queries, own_first, scale, carry, piece):
    top, total, accum = carry
    keys, values = piece
    scores = jnp.einsum("thd,nd->thn", queries, keys, preferred_element_type=jnp.float32) * scale
    query_pos = own_first + jnp.arange(queries.shape[0], dtype=jnp.int32)
    key_pos = jnp.arange(keys.shape[0], dtype=jnp.int32)
    causal = (key_pos[None, :] <= query_pos[:, None])[:, None, :]
    masked = jnp.where(causal, scores, FAR_BELOW)
    new_top = jnp.maximum(top, jnp.max(masked, axis=2))
    weights = jnp.where(causal, jnp.exp(masked - new_top[:, :, None]), 0.0)
    total = jnp.sum(weights, axis=2)
    accum = jnp.einsum(
        "thn,nd->thd", weights.astype(jnp.bfloat16), values, preferred_element_type=jnp.float32
    )
    return (new_top, total, accum)


def body(layer_input, attn_weight, rate_weight, rate_bias, decay_rate, skip_gain):
    tok = layer_input.shape[0]
    kv_local = attn_weight.shape[1]
    heads_local = rate_bias.shape[0]
    group = HEADS // KV_HEADS
    scale = HEAD_DIM ** (-0.5)
    merged = jnp.einsum(
        "td,dkc->tkc",
        layer_input,
        lax.all_gather(attn_weight, "seq", axis=0, tiled=True),
        preferred_element_type=jnp.float32,
    )
    rate_part = jnp.dot(layer_input, rate_weight, preferred_element_type=jnp.float32)
    query_part = merged[:, :, : group * HEAD_DIM].reshape(tok, kv_local * group * HEAD_DIM)
    grp_index = lax.axis_index("grp")
    query_flat, raw = (
        summed_on_arrival(query_part, "grp", 1),
        summed_on_arrival(rate_part, "grp", 1),
    )
    pairs = of_everyone(merged[:, :, group * HEAD_DIM :], "grp")
    kv_index = grp_index * heads_local // group
    pair = lax.dynamic_index_in_dim(pairs, kv_index, 1, keepdims=False)
    keys = pair[:, :HEAD_DIM]
    values = pair[:, HEAD_DIM:].astype(jnp.bfloat16)
    query = query_flat.reshape(tok, heads_local, HEAD_DIM)
    own_first = lax.axis_index("seq") * tok
    cosine, sine = rope_angles(own_first + jnp.arange(tok, dtype=jnp.int32))
    rot_query = rotate(query, cosine, sine).astype(jnp.bfloat16)
    rot_keys = rotate(keys[:, None, :], cosine, sine)[:, 0].astype(jnp.bfloat16)
    start_carry = (
        jnp.full((tok, heads_local), FAR_BELOW, jnp.float32),
        jnp.zeros((tok, heads_local), jnp.float32),
        jnp.zeros((tok, heads_local, HEAD_DIM), jnp.float32),
    )
    top, total, accum = key_absorber(
        rot_query,
        own_first,
        scale,
        start_carry,
        (
            lax.all_gather(rot_keys, "seq", axis=0, tiled=True),
            lax.all_gather(values, "seq", axis=0, tiled=True),
        ),
    )
    teacher = (accum / total[:, :, None]).astype(jnp.bfloat16).reshape(tok, heads_local * HEAD_DIM)
    step = jax.nn.softplus(raw + rate_bias[None, :])
    log_decay = -decay_rate[None, :] * step
    c_all = query.astype(jnp.bfloat16)
    b_all = keys.astype(jnp.bfloat16)
    causal = (
        jnp.arange(STRETCH, dtype=jnp.int32)[:, None]
        >= jnp.arange(STRETCH, dtype=jnp.int32)[None, :]
    )[None]
    state = jnp.zeros((heads_local, HEAD_DIM, HEAD_DIM), jnp.float32)
    before = jnp.zeros((heads_local,), jnp.float32)
    partials = []
    offsets = []
    for index in range(tok // STRETCH):
        first = index * STRETCH
        cpart = c_all[first : first + STRETCH]
        bpart = b_all[first : first + STRETCH]
        xpart = values[first : first + STRETCH]
        decay = log_decay[first : first + STRETCH]
        rate = step[first : first + STRETCH]
        cum = jnp.cumsum(decay, axis=0)
        gram = jnp.einsum("thn,sn->hts", cpart, bpart, preferred_element_type=jnp.float32) * scale
        diff = cum.T[:, :, None] - cum.T[:, None, :]
        mix = jnp.where(
            causal, jnp.exp(jnp.where(causal, diff, -10000.0)) * rate.T[:, None, :] * gram, 0.0
        ).astype(jnp.bfloat16)
        intra = jnp.einsum("hts,sp->thp", mix, xpart, preferred_element_type=jnp.float32)
        carried = state_product(cpart, state) * scale * jnp.exp(cum)[:, :, None]
        weighted = (
            (jnp.exp(cum[-1][None, :] - cum) * rate)[:, :, None]
            * bpart.astype(jnp.float32)[:, None, :]
        ).astype(jnp.bfloat16)
        contribution = jnp.einsum(
            "shn,sp->hnp", weighted, xpart, preferred_element_type=jnp.float32
        )
        state = jnp.exp(cum[-1])[:, None, None] * state + contribution
        partials.append(intra + carried)
        offsets.append(cum + before[None, :])
        before = before + cum[-1]
    totals, states = tuple(
        (
            part.astype(jnp.float32)
            for part in sent_together(
                (before[None, :].astype(jnp.bfloat16), state[None].astype(jnp.bfloat16)),
                "seq",
                0,
                2,
            )
        )
    )
    position = lax.axis_index("seq")
    order = jnp.arange(totals.shape[0], dtype=jnp.int32)
    between = ((order[:, None] < order[None, :]) & (order[None, :] < position)).astype(jnp.float32)
    span = jnp.dot(between, totals, precision=lax.Precision.HIGHEST)
    reach_back = jnp.where(order[:, None] < position, jnp.exp(span), 0.0)
    incoming = jnp.einsum("dh,dhnp->hnp", reach_back, states, precision=lax.Precision.HIGHEST)
    inside = jnp.concatenate(partials, axis=0)
    reach = jnp.exp(jnp.concatenate(offsets, axis=0))
    arriving = state_product(c_all, incoming) * scale * reach[:, :, None]
    skipped = skip_gain[None, :, None] * values.astype(jnp.float32)[:, None, :]
    student = (
        (inside + arriving + skipped).astype(jnp.bfloat16).reshape(tok, heads_local * HEAD_DIM)
    )
    return (teacher, student)


def solution(mesh):
    placed = (
        P("seq", "grp"),
        P(("grp", "seq"), "mdl", None),
        P("grp", "mdl"),
        P(("mdl", "grp")),
        P(("mdl", "grp")),
        P(("mdl", "grp")),
    )
    return jax.shard_map(
        body,
        mesh=mesh,
        in_specs=placed,
        out_specs=(P("seq", ("mdl", "grp")), P("seq", ("mdl", "grp"))),
        check_vma=False,
    )
```

profile of v0, /device:TPU:217, one launch (start us, length us, event | category | flops | bytes accessed | tf_op | source)
XLA Modules:
  0.0 410.9 jit_solution(16741046107734703974)
XLA Ops:
  7.2 2.2 copy.141
  9.4 120.7 %all-gather.6.cloned.1.call-done = bf16[2048,2,1280]{2,0,1:T(8,128)(2,1)} async-done(((bf16[128,2,1280]{2,0,1:T(8,128)(2,1)}), bf16[2048,2,1280]{2,0,1:T(8,128)(2,1)}) %all-gather.6.cloned.1.call-update) | async-done | bytes 10485776 | tf_op jit(solution)/shard_map/all_gather | solution.py:100
  130.2 8.3 %fusion.9 = f32[512,2,1280]{2,0,1:T(8,128)S(1)} fusion(bf16[2048,2,1280]{2,0,1:T(8,128)(2,1)} %all-gather.6.cloned.1.call-done, bf16[512,2048]{1,0:T(8,128)(2,1)S(1)} %copy-done), kind=kOutput, calls=%fused_computation.11 | convolution fusion | flops 5368709120 | bytes 17825792 | tf_op jit(solution)/shard_map/td,dkc->tkc/dot_general | solution.py:97
  138.4 2.3 copy-done.2
  140.8 2.4 broadcast_in_dim.117
  143.2 4.9 %all-to-all-start.1 = ((f32[4,512,2,256]{3,1,2,0:T(8,128)}), f32[4,512,2,256]{3,1,2,0:T(8,128)}, u32[]{:S(2)}, u32[]{:S(2)}) async-start(f32[4,512,2,256]{3,1,2,0:T(8,128)} %broadcast_in_dim.117), calls=%async_computation.1 | async-start | bytes 8388608 | tf_op jit(solution)/shard_map/all_to_all | solution.py:31
  149.5 4.7 %slice.103 = f32[512,2,1024]{2,0,1:T(8,128)} slice(f32[512,2,1280]{2,0,1:T(8,128)} %copy-done.2), slice={[0:512], [0:2], [0:1024]} | slice | bytes 8388608 | tf_op jit(solution)/shard_map/slice | solution.py:104
  154.2 5.4 %copy.142 = f32[512,2,1024]{0,2,1:T(8,128)} copy(f32[512,2,1024]{2,0,1:T(8,128)} %slice.103) | data formatting | bytes 8388608 | tf_op jit(solution)/shard_map/slice | solution.py:104
  159.6 37.3 %all-to-all-done.1 = f32[4,512,2,256]{3,1,2,0:T(8,128)} async-done(((f32[4,512,2,256]{3,1,2,0:T(8,128)}), f32[4,512,2,256]{3,1,2,0:T(8,128)}, u32[]{:S(2)}, u32[]{:S(2)}) %all-to-all-start.1) | async-done | bytes 4194336 | tf_op jit(solution)/shard_map/all_to_all | solution.py:31
  196.9 3.3 all-to-all-start.2
  200.2 2.6 reduce_sum.37
  204.4 4.8 %all-to-all-start = ((f32[4,512,512]{1,2,0:T(8,128)}), f32[4,512,512]{1,2,0:T(8,128)}, u32[]{:S(2)}, u32[]{:S(2)}) async-start(f32[4,512,512]{1,2,0:T(8,128)} %bitcast.174), calls=%async_computation | async-start | bytes 8388608 | tf_op jit(solution)/shard_map/all_to_all | solution.py:25
  209.3 5.2 %iota_compare_fusion = pred[512,8192]{1,0:T(8,128)(4,1)} fusion(s32[512]{0:T(512)S(1)} %iota_add_fusion), kind=kLoop, calls=%fused_computation.7 | loop fusion | flops 4194304 | bytes 4196352 | tf_op jit(solution)/shard_map/le | solution.py:80
  216.9 1.2 reduce-window.16
  218.4 1.2 reduce-window.14
  224.5 31.5 %all-to-all-done = f32[4,512,512]{1,2,0:T(8,128)} async-done(((f32[4,512,512]{1,2,0:T(8,128)}), f32[4,512,512]{1,2,0:T(8,128)}, u32[]{:S(2)}, u32[]{:S(2)}) %all-to-all-start) | async-done | bytes 4194336 | tf_op jit(solution)/shard_map/all_to_all | solution.py:25
  255.9 2.8 reduce_sum.36
  261.1 1.0 fusion.33
  262.4 1.1 fusion.35
  263.4 1.4 pad_maximum_fusion
  265.3 2.6 fusion.31
  267.9 2.6 fusion.30
  270.4 27.0 %fusion = (f32[512,4]{0,1:T(4,128)S(1)}, f32[512,4,8192]{2,0,1:T(8,128)}) fusion(pred[512,8192]{1,0:T(8,128)(4,1)} %iota_compare_fusion, bf16[8192,1,128]{0,2,1:T(8,128)(2,1)} %all-gather.12.cloned.1.call-done, bf16[512,4,64]{2,0,1:T(8,128)(2,1)S(1)} %get-tuple-element.17, bf16[512,4,64]{2,0,1:T(8,128)(2,1)S(1)} %get-tuple-element.16), kind=kOutput, calls=%fused_computation.2 | convolution fusion | flops 4346345472 | bytes 73932800 | tf_op jit(solution)/shard_map/thd,nd->thn/dot_general | solution.py:77
  297.4 23.2 %fusion.1 = f32[512,4]{0,1:T(4,128)S(1)} fusion(f32[512,4,8192]{2,0,1:T(8,128)} %get-tuple-element.43, f32[512,4]{0,1:T(4,128)S(1)} %broadcast_maximum_fusion, pred[512,8192]{1,0:T(8,128)(4,1)} %iota_compare_fusion), kind=kLoop, calls=%fused_computation.3 | loop fusion | flops 83884032 | bytes 71319552 | tf_op jit(solution)/shard_map/reduce_sum | solution.py:84
  320.6 5.8 %all-gather.8.cloned.1.call-done = bf16[8192,128]{0,1:T(8,128)(2,1)} async-done(((bf16[512,128]{0,1:T(8,128)(2,1)}), bf16[8192,128]{0,1:T(8,128)(2,1)}) %all-gather.8.cloned.1.call-update) | async-done | bytes 2097168 | tf_op jit(solution)/shard_map/all_gather | solution.py:132
  326.4 27.3 %divide_convert_fusion = bf16[512,4,128]{0,2,1:T(8,128)(2,1)S(1)} fusion(bf16[8192,128]{0,1:T(8,128)(2,1)} %all-gather.8.cloned.1.call-done, f32[512,4,8192]{2,0,1:T(8,128)} %get-tuple-element.43, f32[512,4]{0,1:T(4,128)S(1)} %broadcast_maximum_fusion, pred[512,8192]{1,0:T(8,128)(4,1)} %iota_compare_fusion, f32[512,4]{0,1:T(4,128)S(1)} %fusion.1), kind=kOutput, calls=%fused_computation.56 | convolution fusion | flops 4379377664 | bytes 73940992 | tf_op jit(solution)/shard_map/thn,nd->thd/dot_general | solution.py:85
  354.7 33.1 %all-gather.10.cloned.1.call-done = bf16[16,4,16385]{2,1,0:T(4,128)(2,1)} async-done(((bf16[1,4,16385]{2,1,0:T(4,128)(2,1)}), bf16[16,4,16385]{2,1,0:T(4,128)(2,1)}) %all-gather.10.cloned.1.call-update) | async-done | bytes 2097296 | tf_op jit(solution)/shard_map/all_gather | solution.py:44
  387.9 4.2 %split.9 = bf16[16,4,16384]{2,1,0:T(4,128)(2,1)} slice(bf16[16,4,16385]{2,1,0:T(4,128)(2,1)} %all-gather.10.cloned.1.call-done), slice={[0:16], [0:4], [1:16385]} | slice | bytes 4194304 | tf_op jit(solution)/shard_map/split | solution.py:45
  392.0 4.8 %reshape.291 = bf16[16,4,128,128]{3,2,1,0:T(8,128)(2,1)} reshape(bf16[16,4,16384]{2,1,0:T(4,128)(2,1)} %split.9) | data formatting | bytes 4194304 | tf_op jit(solution)/shard_map/reshape | solution.py:46
  397.8 3.4 fusion.11
  401.7 1.7 fusion.23
  403.3 1.0 copy.163
  (81 shorter events, 15.9 us)
Async XLA Ops:
  7.2 123.0 %copy-start = (bf16[512,2048]{1,0:T(8,128)(2,1)S(1)}, bf16[512,2048]{1,0:T(8,128)(2,1)}, u32[]{:S(2)}) copy-start(bf16[512,2048]{1,0:T(8,128)(2,1)} %param.6) | copy-start | bytes 6291460
  7.2 123.0 %all-gather.6.cloned.1.call-start = ((), (), s32[]{:S(2)}) async-start(), calls=%async_computation.3 | async-start | bytes 11141120 | tf_op jit(solution)/shard_map/all_gather | solution.py:100
  138.4 2.3 copy-start.2
  140.7 7.4 %copy-start.3 = (bf16[2048,16]{0,1:T(8,128)(2,1)S(1)}, bf16[2048,16]{0,1:T(8,128)(2,1)}, u32[]{:S(2)}) copy-start(bf16[2048,16]{0,1:T(8,128)(2,1)} %param.8) | copy-start | bytes 196612
  143.2 53.6 %all-to-all-start.1 = ((f32[4,512,2,256]{3,1,2,0:T(8,128)}), f32[4,512,2,256]{3,1,2,0:T(8,128)}, u32[]{:S(2)}, u32[]{:S(2)}) async-start(f32[4,512,2,256]{3,1,2,0:T(8,128)} %broadcast_in_dim.117), calls=%async_computation.1 | async-start | bytes 8388608 | tf_op jit(solution)/shard_map/all_to_all | solution.py:31
  196.9 7.5 %all-to-all-start.2 = ((f32[4,512,4]{1,2,0:T(4,128)}), f32[4,512,4]{1,2,0:T(4,128)S(1)}, u32[]{:S(2)}, u32[]{:S(2)}) async-start(f32[4,512,4]{1,2,0:T(4,128)} %bitcast.11), calls=%async_computation.2 | async-start | bytes 65536 | tf_op jit(solution)/shard_map/all_to_all | solution.py:25
  200.1 14.4 %copy-start.6 = (f32[4]{0:T(128)S(1)}, f32[4]{0:T(128)}, u32[]{:S(2)}) copy-start(f32[4]{0:T(128)} %param.10) | copy-start | bytes 52
  200.2 16.6 %copy-start.4 = (f32[4]{0:T(128)S(1)}, f32[4]{0:T(128)}, u32[]{:S(2)}) copy-start(f32[4]{0:T(128)} %param.9) | copy-start | bytes 52
  200.2 70.3 %all-gather.12.cloned.1.call-start = ((), (), s32[]{:S(2)}) async-start(), calls=%async_computation.6 | async-start | bytes 2228224 | tf_op jit(solution)/shard_map/all_gather | solution.py:131
  204.4 51.5 %all-to-all-start = ((f32[4,512,512]{1,2,0:T(8,128)}), f32[4,512,512]{1,2,0:T(8,128)}, u32[]{:S(2)}, u32[]{:S(2)}) async-start(f32[4,512,512]{1,2,0:T(8,128)} %bitcast.174), calls=%async_computation | async-start | bytes 8388608 | tf_op jit(solution)/shard_map/all_to_all | solution.py:25
  209.3 117.2 %all-gather.8.cloned.1.call-start = ((), (), s32[]{:S(2)}) async-start(), calls=%async_computation.4 | async-start | bytes 2228224 | tf_op jit(solution)/shard_map/all_gather | solution.py:132
  222.9 164.9 %all-gather.10.cloned.1.call-start = ((), (), s32[]{:S(2)}) async-start(), calls=%async_computation.5 | async-start | bytes 2245632 | tf_op jit(solution)/shard_map/all_gather | solution.py:44
  320.6 77.0 %copy-start.7 = (pred[16]{0:T(512)(128)(4,1)S(1)}, pred[16]{0:T(512)(128)(4,1)}, u32[]{:S(2)}) copy-start(pred[16]{0:T(512)(128)(4,1)} %iota_compare_fusion.3) | copy-start | bytes 52
  326.4 77.9 %copy-start.1 = (bf16[512,2048]{1,0:T(8,128)(2,1)S(1)}, bf16[512,2048]{1,0:T(8,128)(2,1)}, u32[]{:S(2)}) copy-start(bf16[512,2048]{1,0:T(8,128)(2,1)} %param.6) | copy-start | bytes 6291460
  353.7 47.9 %copy-start.5 = (f32[4]{0:T(128)S(1)}, f32[4]{0:T(128)}, u32[]{:S(2)}) copy-start(f32[4]{0:T(128)} %param.11) | copy-start | bytes 52
Sparse Core Ops, SparseCore 0:
  10.8 119.3 all-gather.5
  204.5 60.6 all-gather.11
  267.7 58.6 all-gather.7
  329.0 58.7 all-gather.9
where the time goes:
time: 419 us; the launch traced here: 411 us
  waiting for transfers between devices  229 us (55%)
  matrix products  78 us (19%)
  other arithmetic  44.8 us (11%)
  local copies, waits for them, and re-layouts  32.1 us (8%)
  between operations  14.1 us (3%)
  starting transfers between devices  13.3 us (3%)
    all_gather x1, waiting for transfers between devices, body(): lax.all_gather(attn_weight, 'seq', axis=0, tiled=True)  121 us
    all_to_all x1, waiting for transfers between devices, copy_for_each(): lax.all_to_all(jnp.broadcast_to(x[None], (count, *x.shape)), axis, 0, 0,...  37.3 us
    all_gather x1, waiting for transfers between devices, sent_together(): out = lax.all_gather(both, axis, axis=dim, tiled=True)  33.1 us
    all_to_all x2, waiting for transfers between devices, summed_on_arrival(): tiles = lax.all_to_all(cut_along(x, dim, count), axis, 0, 0, tiled=True)  31.5 us
    dot_general x1, matrix products, key_absorber(): jnp.einsum('thn,nd->thd', weights.astype(jnp.bfloat16), values, preferred...  27.3 us
    dot_general x1, matrix products, key_absorber(): jnp.einsum('thd,nd->thn', queries, keys, preferred_element_type=jnp.float32)  27 us
    reduce_sum x1, other arithmetic, key_absorber(): total = jnp.sum(weights, axis=2)  23.2 us
    slice x2, local copies, waits for them, and re-layouts, body(): merged[:, :, :group * HEAD_DIM].reshape(tok, kv_local * group * HEAD_DIM)  10.1 us
  transfers between devices with their start and end apart: 7, of which 6 were waited for; matrix products, arithmetic and copies ran while one was open for 30% of the time, Pallas kernels for 0%

commit v1 on v0

v1 whole, which is shorter than its diff:
```python
import functools
import math

import jax
import jax.numpy as jnp
import numpy as np
from jax import lax
from jax.experimental import pallas as pl
from jax.experimental.pallas import tpu as pltpu
from jax.sharding import PartitionSpec as P

HEAD_DIM = 128
STRETCH = 256
ROPE_BASE = 500000.0
FAR_BELOW = -1e30
TOK = 512
LOCAL_HEADS = 4
CHUNKS = 5
COPIES = 11
SCALE = HEAD_DIM**-0.5
LOG2E = math.log2(math.e)
MESH = pl.DeviceIdType.MESH
BF = jnp.bfloat16
F32 = jnp.float32


def places():
    g, s, m = lax.axis_index("grp"), lax.axis_index("seq"), lax.axis_index("mdl")
    zh, y, c = s // 8, (s // 2) % 4, s % 2

    def seq(zh, y, c):
        return zh * 8 + y * 2 + c

    up, down, far = lax.rem(y + 1, 4), lax.rem(y + 3, 4), lax.rem(y + 2, 4)
    return {
        "g": g, "s": s, "zh": zh, "y": y, "c": c,
        "zy": zh * 4 + y,
        "up": up, "down": down, "far": far,
        "R": (g, seq(zh, up, c), m),
        "L": (g, seq(zh, down, c), m),
        "Z": (g, seq(1 - zh, y, c), m),
        "S": (g, seq(zh, y, 1 - c), m),
        "G": [(lax.rem(g + d, 4), s, m) for d in (1, 2, 3)],
    }


def enter(names, p):
    bar = pltpu.get_barrier_semaphore()
    targets = []
    for name in names:
        targets += p[name] if name == "G" else [p[name]]
    for dev in targets:
        pl.semaphore_signal(bar, inc=1, device_id=dev, device_id_type=MESH)
    pl.semaphore_wait(bar, len(targets))


class Gather:
    def __init__(self, buf, ssem, rsem, p, half, up_only):
        self.buf, self.ssem, self.rsem, self.p = buf, ssem, rsem, p
        self.rows = buf.shape[-2]
        self.half, self.up_only = half, up_only

    def copy(self, k, dev, zy, first=None, count=None, core=None):
        c = self.p["c"] if core is None else core
        ref = self.buf.at[c, zy] if first is None else self.buf.at[c, zy, pl.ds(first, count)]
        return pltpu.make_async_remote_copy(
            src_ref=ref, dst_ref=ref, send_sem=self.ssem.at[k], recv_sem=self.rsem.at[k],
            device_id=dev, device_id_type=MESH,
        )

    def four(self, k, zh, core):
        ref = self.buf.at[core, pl.ds(zh * 4, 4)]
        return pltpu.make_async_remote_copy(
            src_ref=ref, dst_ref=ref, send_sem=self.ssem.at[k], recv_sem=self.rsem.at[k],
            device_id=self.p["S"], device_id_type=MESH,
        )

    def only(self, cond, f):
        if self.up_only:
            pl.when(cond)(f)
        else:
            f()

    def base(self, own):
        return (self.p["zh"] if own else 1 - self.p["zh"]) * 4

    def spread(self, own):
        p, k = self.p, 0 if own else 5
        at = self.base(own) + p["y"]
        return self.copy(k, p["R"], at), self.copy(k + 1, p["L"], at)

    def arrive(self, own):
        p, k = self.p, 0 if own else 5
        return (
            self.copy(k, p["R"], self.base(own) + p["down"]),
            self.copy(k + 1, p["L"], self.base(own) + p["up"]),
        )

    def forward(self, own):
        p, k = self.p, 2 if own else 7
        return (
            self.copy(k, p["R"], self.base(own) + p["down"], 0, self.half),
            self.copy(k + 1, p["L"], self.base(own) + p["up"], self.half, self.rows - self.half),
        )

    def halves(self, own):
        p, k = self.p, 2 if own else 7
        return (
            self.copy(k, p["R"], self.base(own) + p["far"], 0, self.half),
            self.copy(k + 1, p["L"], self.base(own) + p["far"], self.half, self.rows - self.half),
        )

    def a(self):
        right, left = self.spread(True)
        right.start()
        left.start()
        self.only(self.p["zh"] == 0, lambda: self.copy(4, self.p["Z"], self.p["zy"]).start())

    def pass_on(self, own):
        for got, on in zip(self.arrive(own), self.forward(own)):
            got.wait_recv()
            on.start()

    def b(self):
        self.pass_on(True)

        def other():
            self.copy(4, self.p["Z"], self.base(False) + self.p["y"]).wait_recv()
            for cp in self.spread(False):
                cp.start()

        self.only(self.p["zh"] == 1, other)

    def finish(self, own):
        for cp in self.halves(own):
            cp.wait_recv()
        self.four(9 if own else 10, self.p["zh"] if own else 1 - self.p["zh"], self.p["c"]).start()

    def c(self):
        self.finish(True)
        self.only(self.p["zh"] == 1, lambda: self.pass_on(False))

    def d(self):
        self.only(self.p["zh"] == 1, lambda: self.finish(False))

    def e(self):
        self.four(9, self.p["zh"], 1 - self.p["c"]).wait_recv()
        self.only(
            self.p["zh"] == 1, lambda: self.four(10, 1 - self.p["zh"], 1 - self.p["c"]).wait_recv()
        )

    def sent(self):
        for cp in (*self.spread(True), *self.forward(True)):
            cp.wait_send()
        self.only(self.p["zh"] == 0, lambda: self.copy(4, self.p["Z"], self.p["zy"]).wait_send())

        def other():
            for cp in (*self.spread(False), *self.forward(False)):
                cp.wait_send()
            self.four(10, 1 - self.p["zh"], self.p["c"]).wait_send()

        self.only(self.p["zh"] == 1, other)
        self.four(9, self.p["zh"], self.p["c"]).wait_send()


def dot(a, b):
    return jnp.dot(a, b, preferred_element_type=F32)


def dot_t(a, b, precision=None):
    return lax.dot_general(
        a, b, (((1,), (1,)), ((), ())), preferred_element_type=F32, precision=precision
    )


def project_kernel(
    x_ref, w_ref, rate_ref, near_ref, base_ref,
    rq_ref, ct_ref, kv_ref, b_ref, raw_ref,
    wg, xp, own, qsend, qrecv, kvsend, kvrecv, rawsend, rawrecv,
    wssem, wrsem, gssem, grsem,
):
    p = places()
    g = p["g"]

    def place(chunk):
        for d in range(4):
            k = d // 2
            first = k * 1280 + (1024 + (d % 2) * 128 if chunk == 0 else (d % 2) * 512 + (chunk - 1) * 128)
            wg[chunk, p["c"], p["zy"], :, d * 128 : d * 128 + 128] = w_ref[:, first : first + 128]

    gathers = [
        Gather(wg.at[n], wssem.at[n], wrsem.at[n], p, 64, False) for n in range(CHUNKS)
    ]
    place(0)
    enter(["R", "L", "Z", "S", "G"], p)
    gathers[0].a()
    place(1)
    gathers[1].a()
    for n in range(2, CHUNKS):
        place(n)

    def tile(source, target, k, d):
        return pltpu.make_async_remote_copy(
            src_ref=source, dst_ref=target, send_sem=gssem.at[k, d], recv_sem=grsem.at[k, d],
            device_id=p["G"][d], device_id_type=MESH,
        )

    def raw_tile(d):
        return tile(rawsend.at[lax.rem(g + d + 1, 4)], rawrecv.at[d], CHUNKS, d)

    def kv_tile(d):
        return tile(kvsend.at[lax.rem(g + d + 1, 4) // 2], kvrecv.at[d], 0, d)

    def q_tile(n, d):
        return tile(qsend.at[n - 1, lax.rem(g + d + 1, 4)], qrecv.at[n - 1, d], n, d)

    def tiles(n):
        return [kv_tile(d) if n == 0 else q_tile(n, d) for d in range(3)]

    raw = dot_t(rate_ref[...], x_ref[...])
    for d in range(4):
        rawsend[d] = jnp.concatenate([raw[4 * d : 4 * d + 4], raw[4 * d : 4 * d + 4]], axis=0)
    for d in range(3):
        raw_tile(d).start()
    for core in range(2):
        for zy in range(8):
            src = (zy * 2 + core) * 128
            xp[core, :, zy * 128 : zy * 128 + 128] = x_ref[:, src : src + 128]

    def angles():
        near_c, near_s = near_ref[0], near_ref[1]
        far_c, far_s = base_ref[0, pl.ds(p["s"], 1), :], base_ref[1, pl.ds(p["s"], 1), :]
        sign = jnp.where(lax.broadcasted_iota(jnp.int32, (1, HEAD_DIM), 1) < HEAD_DIM // 2, -1.0, 1.0)
        cosine = near_c * far_c - near_s * far_s
        sine = (near_s * far_c + near_c * far_s) * sign
        return cosine, sine

    def rotate(u):
        cosine, sine = angles()
        return u * cosine + pltpu.roll(u, HEAD_DIM // 2, 1) * sine

    def multiply(n):
        gathers[n].e()
        out = sum(dot(xp[core], wg[n, core].reshape(1024, 512)) for core in range(2))
        for d in range(4):
            part = out[:, d * 128 : d * 128 + 128]
            own[n % 2, d] = part
            if n == 0:
                kvsend[d // 2, :, (d % 2) * 128 : (d % 2) * 128 + 128] = part.astype(BF)
            else:
                qsend[n - 1, d] = part.astype(BF)
        for cp in tiles(n):
            cp.start()

    def settle(n):
        for cp in tiles(n):
            cp.wait_recv()
        if n == 0:
            k = g // 2
            keys, value = own[0, 2 * k], own[0, 2 * k + 1]
            for d in range(3):
                keys = keys + kvrecv[d, :, :128].astype(F32)
                value = value + kvrecv[d, :, 128:].astype(F32)
            kv_ref[:, :128] = rotate(keys).astype(BF)
            kv_ref[:, 128:] = value.astype(BF)
            b_ref[...] = keys.astype(BF)
        else:
            query = own[n % 2, g]
            for d in range(3):
                query = query + qrecv[n - 1, d].astype(F32)
            ct_ref[n - 1] = query.astype(BF)
            rq_ref[n - 1] = (rotate(query) * (SCALE * LOG2E)).astype(BF)

    for step in range(CHUNKS + 4):
        for stage, n in (("d", step - 2), ("c", step - 1), ("b", step)):
            if 0 <= n < CHUNKS:
                getattr(gathers[n], stage)()
        if step + 2 < CHUNKS:
            gathers[step + 2].a()
        if 0 <= step - 2 < CHUNKS:
            multiply(step - 2)
        if 0 <= step - 3 < CHUNKS:
            settle(step - 3)
    total = rawsend[g]
    for d in range(3):
        raw_tile(d).wait_recv()
        total = total + rawrecv[d]
    raw_ref[...] = total
    for n in range(CHUNKS):
        gathers[n].sent()
        for cp in tiles(n):
            cp.wait_send()
    for d in range(3):
        raw_tile(d).wait_send()


def attend_kernel(
    rq_ref, ct_ref, kv_ref, b_ref, raw_ref, bias_ref, rate_ref, skip_ref,
    teacher_ref, student_ref,
    kvall, stall, acc, top, contrib, ssem, rsem,
):
    p = places()
    s = p["s"]
    kv = Gather(kvall, ssem.at[0], rsem.at[0], p, 256, True)
    st = Gather(stall, ssem.at[1], rsem.at[1], p, 256, True)
    kvall[p["c"], p["zy"]] = kv_ref[...]
    enter(["R", "L", "Z", "S"], p)
    kv.a()

    row = lax.broadcasted_iota(jnp.int32, (8, TOK), 0)

    def per_head(ref):
        out = jnp.full((8, TOK), ref[0], F32)
        for h in range(1, LOCAL_HEADS):
            out = jnp.where(row % LOCAL_HEADS == h, ref[h], out)
        return out

    arg = raw_ref[...] + per_head(bias_ref)
    step = jnp.maximum(arg, 0.0) + jnp.log1p(jnp.exp(-jnp.abs(arg)))
    decay = -per_head(rate_ref) * step
    from_t = lax.broadcasted_iota(jnp.int32, (STRETCH, STRETCH), 0)
    from_s = lax.broadcasted_iota(jnp.int32, (STRETCH, STRETCH), 1)
    causal = from_s <= from_t
    lower = causal.astype(F32)
    upper = (from_t <= from_s).astype(F32)
    pieces = []
    for i in range(2):
        part = decay[:, i * STRETCH : (i + 1) * STRETCH]
        cum_row = jnp.dot(part, upper, preferred_element_type=F32, precision=lax.Precision.HIGHEST)
        cum_col = dot_t(lower, part, lax.Precision.HIGHEST)
        pieces.append((cum_row, cum_col, step[:, i * STRETCH : (i + 1) * STRETCH]))
    values = [kv_ref[i * STRETCH : (i + 1) * STRETCH, 128:] for i in range(2)]
    bterm = [b_ref[i * STRETCH : (i + 1) * STRETCH] for i in range(2)]
    ends = [jnp.exp(jnp.broadcast_to(pieces[i][0][:, STRETCH - 1 :], (8, HEAD_DIM))) for i in range(2)]
    turned = [bterm[i].astype(F32).T for i in range(2)]
    for i in range(2):
        cum_row, _, rate = pieces[i]
        weight = jnp.exp(cum_row[:, STRETCH - 1 :] - cum_row) * rate
        for h in range(LOCAL_HEADS):
            contrib[i, h] = dot((turned[i] * weight[h : h + 1]).astype(BF), values[i])
    for h in range(LOCAL_HEADS):
        local = ends[1][h : h + 1] * contrib[0, h] + contrib[1, h]
        stall[p["c"], p["zy"], h * 128 : h * 128 + 128] = local.astype(BF)
    both = ends[0] * ends[1]
    high = both.astype(BF)
    low = (both - high.astype(F32)).astype(BF)
    stall[p["c"], p["zy"], 512:528] = jnp.concatenate([high, low], axis=0)
    st.a()
    kv.b()
    st.b()

    skips = [skip_ref[h] for h in range(LOCAL_HEADS)]
    for i in range(2):
        cum_row, cum_col, rate = pieces[i]
        rows = slice(i * STRETCH, (i + 1) * STRETCH)
        for h in range(LOCAL_HEADS):
            gram = dot_t(ct_ref[h, rows], bterm[i])
            diff = cum_col[:, h : h + 1] - cum_row[h : h + 1]
            mix = jnp.exp(jnp.where(causal, diff, FAR_BELOW)) * (rate[h : h + 1] * SCALE) * gram
            inside = dot(mix.astype(BF), values[i])
            acc[h, rows, :128] = inside + skips[h] * values[i].astype(F32)
    kv.c()
    st.c()
    kv.d()
    st.d()
    st.e()

    def advance(d, carried):
        block = stall.at[d % 2, d // 2]
        tail = block[512:528].astype(F32)
        total = tail[0:8] + tail[8:16]
        return tuple(
            total[h : h + 1] * carried[h] + block[h * 128 : h * 128 + 128].astype(F32)
            for h in range(LOCAL_HEADS)
        )

    zero = jnp.zeros((HEAD_DIM, HEAD_DIM), F32)
    incoming = lax.fori_loop(0, s, advance, (zero,) * LOCAL_HEADS)
    for i in range(2):
        _, cum_col, _ = pieces[i]
        rows = slice(i * STRETCH, (i + 1) * STRETCH)
        reach = jnp.exp(cum_col) * SCALE
        for h in range(LOCAL_HEADS):
            state = incoming[h] if i == 0 else ends[0][h : h + 1] * incoming[h] + contrib[0, h]
            carried = dot(ct_ref[h, rows], state.astype(BF))
            out = acc[h, rows, :128] + reach[:, h : h + 1] * carried
            student_ref[rows, h * 128 : h * 128 + 128] = out.astype(BF)

    kv.e()
    ones = jnp.ones((TOK, HEAD_DIM), BF)

    def absorb(keys, vals, masked, first):
        wide = jnp.concatenate([vals, ones], axis=1)
        for h in range(LOCAL_HEADS):
            for i in range(2):
                rows = slice(i * STRETCH, (i + 1) * STRETCH)
                scores = dot_t(rq_ref[h, rows], keys)
                if masked:
                    at_t = lax.broadcasted_iota(jnp.int32, scores.shape, 0) + i * STRETCH
                    at_u = lax.broadcasted_iota(jnp.int32, scores.shape, 1)
                    scores = jnp.where(at_u <= at_t, scores, FAR_BELOW)
                high = jnp.max(scores, axis=1, keepdims=True)
                if first:
                    now = jnp.broadcast_to(high, (STRETCH, 128))
                else:
                    now = jnp.maximum(top[h, rows], high)
                weights = jnp.exp2(scores - now[:, :1]).astype(BF)
                mixed = dot(weights, wide)
                if not first:
                    shrink = jnp.exp2(top[h, rows] - now)
                    mixed = mixed + acc[h, rows] * jnp.concatenate([shrink, shrink], axis=1)
                acc[h, rows] = mixed
                top[h, rows] = now

    absorb(kv_ref[:, :128], kv_ref[:, 128:], True, True)

    def visit(j, carry):
        block = kvall.at[j % 2, j // 2]
        absorb(block[:, :128], block[:, 128:], False, False)
        return carry

    lax.fori_loop(0, s, visit, 0)
    for h in range(LOCAL_HEADS):
        done = acc[h]
        teacher_ref[:, h * 128 : h * 128 + 128] = (done[:, :128] / done[:, 128:]).astype(BF)
    kv.sent()
    st.sent()


def tables():
    half = HEAD_DIM // 2
    freq = ROPE_BASE ** (-2.0 * np.arange(half) / HEAD_DIM)
    freq = np.concatenate([freq, freq])
    near = np.arange(TOK)[:, None] * freq[None]
    base = (np.arange(16) * TOK)[:, None] * freq[None]
    return (
        np.stack([np.cos(near), np.sin(near)]).astype(np.float32),
        np.stack([np.cos(base), np.sin(base)]).astype(np.float32),
    )


def body(layer_input, attn_weight, rate_weight, rate_bias, decay_rate, skip_gain):
    vmem = pl.BlockSpec(memory_space=pltpu.VMEM)
    smem = pl.BlockSpec(memory_space=pltpu.SMEM)
    dma = pltpu.SemaphoreType.DMA
    near, base = tables()
    heads = (LOCAL_HEADS, TOK, HEAD_DIM)
    rq, ct, kv, bterm, raw = pl.pallas_call(
        project_kernel,
        name="project",
        out_shape=(
            jax.ShapeDtypeStruct(heads, BF),
            jax.ShapeDtypeStruct(heads, BF),
            jax.ShapeDtypeStruct((TOK, 256), BF),
            jax.ShapeDtypeStruct((TOK, HEAD_DIM), BF),
            jax.ShapeDtypeStruct((8, TOK), F32),
        ),
        in_specs=[vmem] * 5,
        out_specs=(vmem,) * 5,
        scratch_shapes=[
            pltpu.VMEM((CHUNKS, 2, 8, 128, 512), BF),
            pltpu.VMEM((2, TOK, 1024), BF),
            pltpu.VMEM((2, 4, TOK, 128), F32),
            pltpu.VMEM((4, 4, TOK, 128), BF),
            pltpu.VMEM((4, 3, TOK, 128), BF),
            pltpu.VMEM((2, TOK, 256), BF),
            pltpu.VMEM((3, TOK, 256), BF),
            pltpu.VMEM((4, 8, TOK), F32),
            pltpu.VMEM((3, 8, TOK), F32),
            dma((CHUNKS, COPIES)),
            dma((CHUNKS, COPIES)),
            dma((CHUNKS + 1, 3)),
            dma((CHUNKS + 1, 3)),
        ],
        compiler_params=pltpu.CompilerParams(
            collective_id=0, has_side_effects=True, vmem_limit_bytes=56 * 2**20
        ),
    )(layer_input, attn_weight.reshape(128, 2560), rate_weight.T, jnp.asarray(near), jnp.asarray(base))
    return pl.pallas_call(
        attend_kernel,
        name="attend",
        out_shape=(
            jax.ShapeDtypeStruct((TOK, 512), BF),
            jax.ShapeDtypeStruct((TOK, 512), BF),
        ),
        in_specs=[vmem] * 5 + [smem] * 3,
        out_specs=(vmem, vmem),
        scratch_shapes=[
            pltpu.VMEM((2, 8, TOK, 256), BF),
            pltpu.VMEM((2, 8, 528, 128), BF),
            pltpu.VMEM((LOCAL_HEADS, TOK, 256), F32),
            pltpu.VMEM((LOCAL_HEADS, TOK, 128), F32),
            pltpu.VMEM((2, LOCAL_HEADS, HEAD_DIM, HEAD_DIM), F32),
            dma((2, COPIES)),
            dma((2, COPIES)),
        ],
        compiler_params=pltpu.CompilerParams(
            collective_id=1, has_side_effects=True, vmem_limit_bytes=56 * 2**20
        ),
    )(rq, ct, kv, bterm, raw, rate_bias, decay_rate, skip_gain)


def solution(mesh):
    placed = (
        P("seq", "grp"),
        P(("grp", "seq"), "mdl", None),
        P("grp", "mdl"),
        P(("mdl", "grp")),
        P(("mdl", "grp")),
        P(("mdl", "grp")),
    )
    return jax.shard_map(
        body,
        mesh=mesh,
        in_specs=placed,
        out_specs=(P("seq", ("mdl", "grp")), P("seq", ("mdl", "grp"))),
        check_vma=False,
    )
```

time: 419 us -> 157 us (0.37); the launches traced: 411 us -> 157 us
  waiting for transfers between devices: 229 us -> 0 us
  Pallas kernels: 0 us -> 150 us
  matrix products: 78 us -> 0 us
  other arithmetic: 44.8 us -> 0 us
  local copies, waits for them, and re-layouts: 32.1 us -> 5.75 us
  between operations: 14.1 us -> 0.65 us
  starting transfers between devices: 13.3 us -> 0 us
    all_gather x4 -> x0, waiting for transfers between devices: 160 us -> none  [the longest x1 121 us: body(): lax.all_gather(attn_weight, 'seq', axis=0, tiled=True)]
    pallas_call x0 -> x2, Pallas kernels: none -> 150 us  [the longest x1 75.7 us: body(): pl.pallas_call(attend_kernel, name='attend', out_shape=(jax.ShapeDtypeStr...]
    dot_general x15 -> x0, matrix products: 78 us -> none  [the longest x1 27.3 us: key_absorber(): jnp.einsum('thn,nd->thd', weights.astype(jnp.bfloat16), values, preferred...]
    all_to_all x3 -> x0, waiting for transfers between devices: 68.9 us -> none  [the longest x1 37.3 us: copy_for_each(): lax.all_to_all(jnp.broadcast_to(x[None], (count, *x.shape)), axis, 0, 0,...]
    reduce_sum x4 -> x0, other arithmetic: 28.6 us -> none  [the longest x1 23.2 us: key_absorber(): total = jnp.sum(weights, axis=2)]
    all_to_all x3 -> x0, starting transfers between devices: 13 us -> none  [the longest x2 8.11 us: summed_on_arrival(): tiles = lax.all_to_all(cut_along(x, dim, count), axis, 0, 0, tiled=True)]
    slice x6 -> x0, local copies, waits for them, and re-layouts: 10.3 us -> none  [the longest x2 10.1 us: body(): merged[:, :, :group * HEAD_DIM].reshape(tok, kv_local * group * HEAD_DIM)]
    reshape x5 -> x0, local copies, waits for them, and re-layouts: 5.81 us -> none  [the longest x1 4.78 us: sent_together(): b.reshape(*out.shape[:along], *a.shape[along:])]
  transfers between devices with their start and end apart: 7 -> 0, of which waited for: 6 -> 0; matrix products, arithmetic and copies ran while one was open for 30% -> 0% of each run, Pallas kernels for 0% -> 0%
where the time goes in v1:
time: 157 us
  Pallas kernels  150 us (96%)
  local copies, waits for them, and re-layouts  5.75 us (4%)
    pallas_call x1, Pallas kernels, body(): pl.pallas_call(attend_kernel, name='attend', out_shape=(jax.ShapeDtypeStr...  75.7 us
    pallas_call x1, Pallas kernels, body(): pl.pallas_call(project_kernel, name='project', out_shape=(jax.ShapeDtypeS...  74.4 us
    unnamed x3, local copies, waits for them, and re-layouts  5.75 us

profile of v1, /device:TPU:217, one launch (start us, length us, event | category | flops | bytes accessed | tf_op | source)
XLA Modules:
  0.0 156.6 jit_solution(5811747518376124888)
XLA Ops:
  0.6 2.0 %copy.10 = bf16[16,8,2,1280]{3,1,2,0:T(8,128)(2,1)} copy(bf16[16,8,2,1280]{3,2,1,0:T(2,128)(2,1)} %bitcast.4) | data formatting | bytes 1310720
  2.6 74.4 %project.1 = (bf16[4,512,128]{2,1,0:T(8,128)(2,1)}, bf16[4,512,128]{2,1,0:T(8,128)(2,1)}, bf16[512,256]{1,0:T(8,128)(2,1)}, bf16[512,128]{1,0:T(8,128)(2,1)}, f32[8,512]{1,0:T(8,128)}) custom-call(bf16[512,2048]{1,0:T(8,128)(2,1)} %x_ref.1, bf16[128,2560]{1,0:T(8,128)(2,1)} %bitcast.3, bf16[16,2048]{1,0:T(8,128)(2,1)} %bitcast.5, ...), custom_call_target="tpu_custom_call" | custom-call | tf_op jit(solution)/shard_map/project/pallas_call | solution.py:448
  77.1 75.7 %attend.1 = (bf16[512,512]{1,0:T(8,128)(2,1)}, bf16[512,512]{1,0:T(8,128)(2,1)}) custom-call(bf16[4,512,128]{2,1,0:T(8,128)(2,1)} %get-tuple-element.7.rq_ref, bf16[4,512,128]{2,1,0:T(8,128)(2,1)} %get-tuple-element.8.ct_ref, bf16[512,256]{1,0:T(8,128)(2,1)} %get-tuple-element.9.kv_ref, bf16[512,128]{1,0:T(8,128)(2,1)} %get-tuple-element.10.b_ref, ...), custom_call_target="tpu_custom_call" | custom-call | tf_op jit(solution)/shard_map/attend/pallas_call | solution.py:479
  152.8 1.9 %copy.13 = bf16[512,512]{1,0:T(8,128)(2,1)} copy(bf16[512,512]{1,0:T(8,128)(2,1)} %get-tuple-element.14) | data formatting | bytes 1048576
  154.7 1.9 %copy.14 = bf16[512,512]{1,0:T(8,128)(2,1)} copy(bf16[512,512]{1,0:T(8,128)(2,1)} %get-tuple-element.15) | data formatting | bytes 1048576

commit v2 on v1

v2 whole, which is shorter than its diff:
```python
import functools
import math

import jax
import jax.numpy as jnp
import numpy as np
from jax import lax
from jax.experimental import pallas as pl
from jax.experimental.pallas import tpu as pltpu
from jax.sharding import PartitionSpec as P

HEAD_DIM = 128
STRETCH = 256
ROPE_BASE = 500000.0
FAR_BELOW = -1e30
TOK = 512
LOCAL_HEADS = 4
CHUNKS = 5
COPIES = 11
HALF = 256
SCALE = HEAD_DIM**-0.5
LOG2E = math.log2(math.e)
MESH = pl.DeviceIdType.MESH
BF = jnp.bfloat16
F32 = jnp.float32


def places():
    g, s, m = lax.axis_index("grp"), lax.axis_index("seq"), lax.axis_index("mdl")
    zh, y, c = s // 8, (s // 2) % 4, s % 2

    def seq(zh, y, c):
        return zh * 8 + y * 2 + c

    up, down, far = lax.rem(y + 1, 4), lax.rem(y + 3, 4), lax.rem(y + 2, 4)
    return {
        "g": g, "s": s, "zh": zh, "y": y, "c": c,
        "zy": zh * 4 + y,
        "up": up, "down": down, "far": far,
        "R": (g, seq(zh, up, c), m),
        "L": (g, seq(zh, down, c), m),
        "Z": (g, seq(1 - zh, y, c), m),
        "S": (g, seq(zh, y, 1 - c), m),
        "G": [(lax.rem(g + d, 4), s, m) for d in (1, 2, 3)],
    }


def enter(names, p):
    bar = pltpu.get_barrier_semaphore()
    targets = []
    for name in names:
        targets += p[name] if name == "G" else [p[name]]
    for dev in targets:
        pl.semaphore_signal(bar, inc=1, device_id=dev, device_id_type=MESH)
    pl.semaphore_wait(bar, len(targets))


class Gather:
    def __init__(self, buf, ssem, rsem, p, half):
        self.buf, self.ssem, self.rsem, self.p = buf, ssem, rsem, p
        self.rows, self.half = buf.shape[-2], half

    def remote(self, k, ref, dev):
        return pltpu.make_async_remote_copy(
            src_ref=ref, dst_ref=ref, send_sem=self.ssem.at[k], recv_sem=self.rsem.at[k],
            device_id=dev, device_id_type=MESH,
        )

    def copy(self, k, dev, zy, first=None, count=None):
        c = self.p["c"]
        ref = self.buf.at[c, zy] if first is None else self.buf.at[c, zy, pl.ds(first, count)]
        return self.remote(k, ref, dev)

    def four(self, k, own, core):
        return self.remote(k, self.buf.at[core, pl.ds(self.base(own), 4)], self.p["S"])

    def base(self, own):
        return (self.p["zh"] if own else 1 - self.p["zh"]) * 4

    def spread(self, own):
        p, k = self.p, 0 if own else 5
        at = self.base(own) + p["y"]
        return self.copy(k, p["R"], at), self.copy(k + 1, p["L"], at)

    def arrive(self, own):
        p, k = self.p, 0 if own else 5
        return (
            self.copy(k, p["R"], self.base(own) + p["down"]),
            self.copy(k + 1, p["L"], self.base(own) + p["up"]),
        )

    def pair(self, own, left, right):
        p, k = self.p, 2 if own else 7
        return (
            self.copy(k, p["R"], self.base(own) + left, 0, self.half),
            self.copy(k + 1, p["L"], self.base(own) + right, self.half, self.rows - self.half),
        )

    def forward(self, own):
        return self.pair(own, self.p["down"], self.p["up"])

    def halves(self, own):
        return self.pair(own, self.p["far"], self.p["far"])

    def across(self, own):
        return self.copy(4, self.p["Z"], self.base(own) + self.p["y"])

    def a(self):
        for cp in self.spread(True):
            cp.start()
        self.across(True).start()

    def pass_on(self, own):
        for got, on in zip(self.arrive(own), self.forward(own)):
            got.wait_recv()
            on.start()

    def b(self):
        self.pass_on(True)
        self.across(False).wait_recv()
        for cp in self.spread(False):
            cp.start()

    def finish(self, own):
        for cp in self.halves(own):
            cp.wait_recv()
        self.four(9 if own else 10, own, self.p["c"]).start()

    def c(self):
        self.finish(True)
        self.pass_on(False)

    def d(self):
        self.finish(False)

    def e(self):
        for own in (True, False):
            self.four(9 if own else 10, own, 1 - self.p["c"]).wait_recv()

    def sent(self):
        for own in (True, False):
            for cp in (*self.spread(own), *self.forward(own)):
                cp.wait_send()
            self.four(9 if own else 10, own, self.p["c"]).wait_send()
        self.across(True).wait_send()


class Earlier(Gather):
    def lift(self, n):
        at = [self.p["y"], self.p["down"], self.p["up"], self.p["far"]][n]
        return self.copy(4 + n, self.p["Z"], at)

    def low(self, f):
        pl.when(self.p["zh"] == 0)(f)

    def high(self, f):
        pl.when(self.p["zh"] == 1)(f)

    def a(self):
        for cp in self.spread(True):
            cp.start()
        self.low(lambda: self.lift(0).start())

    def b(self):
        self.pass_on(True)

        def send():
            self.lift(1).start()
            self.lift(2).start()

        self.low(send)

    def c(self):
        self.finish(True)
        self.low(lambda: self.lift(3).start())

    def near(self):
        self.four(9, True, 1 - self.p["c"]).wait_recv()

    def d(self):
        def hand():
            for n in range(4):
                self.lift(n).wait_recv()
            self.four(10, False, self.p["c"]).start()

        self.high(hand)

    def e(self):
        self.high(lambda: self.four(10, False, 1 - self.p["c"]).wait_recv())

    def sent(self):
        for cp in (*self.spread(True), *self.forward(True)):
            cp.wait_send()
        self.four(9, True, self.p["c"]).wait_send()

        def lifted():
            for n in range(4):
                self.lift(n).wait_send()

        self.low(lifted)
        self.high(lambda: self.four(10, False, self.p["c"]).wait_send())


def dot(a, b):
    return jnp.dot(a, b, preferred_element_type=F32)


def dot_t(a, b, precision=None):
    return lax.dot_general(
        a, b, (((1,), (1,)), ((), ())), preferred_element_type=F32, precision=precision
    )


def window_kernel(
    x_ref, w_ref, rate_w_ref, near_ref, base_ref, bias_ref, rate_ref, skip_ref,
    teacher_ref, student_ref,
    wg, xp, own, qsend, qrecv, kvsend, kvrecv, rawsend, rawrecv,
    kvall, stall, sx, rq, ct, vrow, brow, contrib, inner, acc, top,
    wssem, wrsem, gssem, grsem, kssem, krsem, xssem, xrsem,
):
    p = places()
    g, s, zh, c, zy = p["g"], p["s"], p["zh"], p["c"], p["zy"]
    gathers = [Gather(wg.at[n], wssem.at[n], wrsem.at[n], p, 64) for n in range(CHUNKS)]
    kv = Earlier(kvall, kssem.at[0], krsem.at[0], p, 128)
    st = Earlier(stall, kssem.at[1], krsem.at[1], p, 128)

    def place(chunk):
        for d in range(4):
            k = d // 2
            first = k * 1280 + (1024 + (d % 2) * 128 if chunk == 0 else (d % 2) * 512 + (chunk - 1) * 128)
            wg[chunk, c, zy, :, d * 128 : d * 128 + 128] = w_ref[:, first : first + 128]

    def tile(source, target, k, d):
        return pltpu.make_async_remote_copy(
            src_ref=source, dst_ref=target, send_sem=gssem.at[k, d], recv_sem=grsem.at[k, d],
            device_id=p["G"][d], device_id_type=MESH,
        )

    def raw_tile(d):
        return tile(rawsend.at[lax.rem(g + d + 1, 4)], rawrecv.at[d], CHUNKS, d)

    def tiles(n):
        if n == 0:
            return [tile(kvsend.at[lax.rem(g + d + 1, 4) // 2], kvrecv.at[d], 0, d) for d in range(3)]
        return [tile(qsend.at[n - 1, lax.rem(g + d + 1, 4)], qrecv.at[n - 1, d], n, d) for d in range(3)]

    def rotate(u):
        near_c, near_s = near_ref[0], near_ref[1]
        far_c, far_s = base_ref[0, pl.ds(s, 1), :], base_ref[1, pl.ds(s, 1), :]
        lane = lax.broadcasted_iota(jnp.int32, (1, HEAD_DIM), 1)
        sign = jnp.where(lane < HEAD_DIM // 2, -1.0, 1.0)
        cosine = near_c * far_c - near_s * far_s
        sine = (near_s * far_c + near_c * far_s) * sign
        return u * cosine + pltpu.roll(u, HEAD_DIM // 2, 1) * sine

    def multiply(n):
        gathers[n].e()
        out = sum(dot(xp[core], wg[n, core].reshape(1024, 512)) for core in range(2))
        for d in range(4):
            part = out[:, d * 128 : d * 128 + 128]
            own[n % 2, d] = part
            if n == 0:
                kvsend[d // 2, :, (d % 2) * 128 : (d % 2) * 128 + 128] = part.astype(BF)
            else:
                qsend[n - 1, d] = part.astype(BF)
        for cp in tiles(n):
            cp.start()

    def settle(n):
        for cp in tiles(n):
            cp.wait_recv()
        if n == 0:
            k = g // 2
            keys, value = own[0, 2 * k], own[0, 2 * k + 1]
            for d in range(3):
                keys = keys + kvrecv[d, :, :128].astype(F32)
                value = value + kvrecv[d, :, 128:].astype(F32)
            turned = rotate(keys).astype(BF)
            for i in range(4):
                kvall[c, zy, :128, i * 128 : i * 128 + 128] = turned[i * 128 : i * 128 + 128]
            kvall[c, zy, 128:] = value.T.astype(BF)
            vrow[...] = value.astype(BF)
            brow[...] = keys.astype(BF)
        else:
            query = own[n % 2, g]
            for d in range(3):
                query = query + qrecv[n - 1, d].astype(F32)
            ct[n - 1] = query.astype(BF)
            rq[n - 1] = (rotate(query) * (SCALE * LOG2E)).astype(BF)

    row = lax.broadcasted_iota(jnp.int32, (8, TOK), 0)

    def per_head(ref):
        out = jnp.full((8, TOK), ref[0], F32)
        for h in range(1, LOCAL_HEADS):
            out = jnp.where(row % LOCAL_HEADS == h, ref[h], out)
        return out

    from_t = lax.broadcasted_iota(jnp.int32, (STRETCH, STRETCH), 0)
    from_s = lax.broadcasted_iota(jnp.int32, (STRETCH, STRETCH), 1)
    causal = from_s <= from_t
    rows_of = [slice(i * STRETCH, (i + 1) * STRETCH) for i in range(2)]

    def decays():
        total = rawsend[g]
        for d in range(3):
            raw_tile(d).wait_recv()
            total = total + rawrecv[d]
        arg = total + per_head(bias_ref)
        step = jnp.maximum(arg, 0.0) + jnp.log1p(jnp.exp(-jnp.abs(arg)))
        decay = -per_head(rate_ref) * step
        lower = causal.astype(F32)
        upper = (from_t <= from_s).astype(F32)
        pieces = []
        for i in range(2):
            part = decay[:, rows_of[i]]
            cum_row = jnp.dot(part, upper, preferred_element_type=F32, precision=lax.Precision.HIGHEST)
            cum_col = dot_t(lower, part, lax.Precision.HIGHEST)
            end = jnp.exp(jnp.broadcast_to(cum_row[:, STRETCH - 1 :], (8, HEAD_DIM)))
            pieces.append((cum_row, cum_col, step[:, rows_of[i]], end))
        return pieces

    def swap():
        return pltpu.make_async_remote_copy(
            src_ref=sx.at[c], dst_ref=sx.at[c], send_sem=xssem, recv_sem=xrsem,
            device_id=p["S"], device_id_type=MESH,
        )

    def swapped():
        return pltpu.make_async_remote_copy(
            src_ref=sx.at[1 - c], dst_ref=sx.at[1 - c], send_sem=xssem, recv_sem=xrsem,
            device_id=p["S"], device_id_type=MESH,
        )

    def split(value):
        high = value.astype(BF)
        return jnp.concatenate([high, (value - high.astype(F32)).astype(BF)], axis=0)

    def local_state(pieces):
        for i in range(2):
            cum_row, _, rate, _ = pieces[i]
            turned = brow[rows_of[i]].astype(F32).T
            weight = jnp.exp(cum_row[:, STRETCH - 1 :] - cum_row) * rate
            for h in range(LOCAL_HEADS):
                contrib[i, h] = dot((turned * weight[h : h + 1]).astype(BF), vrow[rows_of[i]])
        for h in range(LOCAL_HEADS):
            local = pieces[1][3][h : h + 1] * contrib[0, h] + contrib[1, h]
            sx[c, h * 128 : h * 128 + 128] = local.astype(BF)
        sx[c, 512:528] = split(pieces[0][3] * pieces[1][3])
        swap().start()

    def whole(ref, first):
        both = ref[first : first + 16].astype(F32)
        return both[:8] + both[8:]

    def chip_state():
        swapped().wait_recv()
        first, second = whole(sx.at[0], 512), whole(sx.at[1], 512)
        for k in range(2):
            at = pl.ds(pl.multiple_of(c * 256 + k * 128, 128), 128)
            decay = jnp.where(c == 0, second[k : k + 1], second[k + 2 : k + 3])
            both = decay * sx[0, at].astype(F32) + sx[1, at].astype(F32)
            stall[c, zy, k * 128 : k * 128 + 128] = both.astype(BF)
        stall[c, zy, 256:272] = split(first * second)

    def inside(pieces, h):
        for i in range(2):
            cum_row, cum_col, rate, _ = pieces[i]
            gram = dot_t(ct[h, rows_of[i]], brow[rows_of[i]])
            diff = cum_col[:, h : h + 1] - cum_row[h : h + 1]
            mix = jnp.exp(jnp.where(causal, diff, FAR_BELOW)) * (rate[h : h + 1] * SCALE) * gram
            value = vrow[rows_of[i]]
            inner[h, rows_of[i]] = dot(mix.astype(BF), value) + skip_ref[h] * value.astype(F32)

    def arriving():
        def advance(d, carried):
            blocks = [stall.at[k, d] for k in range(2)]
            total = whole(blocks[0], 256)
            return tuple(
                total[h : h + 1] * carried[h]
                + blocks[h // 2][h % 2 * 128 : h % 2 * 128 + 128].astype(F32)
                for h in range(LOCAL_HEADS)
            )

        zero = jnp.zeros((HEAD_DIM, HEAD_DIM), F32)
        carried = lax.fori_loop(0, zy, advance, (zero,) * LOCAL_HEADS)
        first = whole(sx.at[0], 512)
        return [
            jnp.where(
                c == 0, carried[h],
                first[h : h + 1] * carried[h] + sx[0, h * 128 : h * 128 + 128].astype(F32),
            )
            for h in range(LOCAL_HEADS)
        ]

    def student(pieces, incoming, h):
        for i in range(2):
            reach = jnp.exp(pieces[i][1]) * SCALE
            state = incoming[h] if i == 0 else pieces[0][3][h : h + 1] * incoming[h] + contrib[0, h]
            carried = dot(ct[h, rows_of[i]], state.astype(BF))
            out = inner[h, rows_of[i]] + reach[:, h : h + 1] * carried
            student_ref[rows_of[i], h * 128 : h * 128 + 128] = out.astype(BF)

    ones = jnp.ones((16, TOK), BF)

    def absorb(blocks, heads, diagonal=False):
        todo = [(b, h, i) for b in range(len(blocks)) for h in heads for i in range(TOK // HALF)]

        def scores(n):
            b, h, i = todo[n]
            keys = jnp.concatenate([blocks[b][:128, k * 128 : k * 128 + 128] for k in range(4)], axis=0)
            out = dot_t(keys, rq[h, i * HALF : i * HALF + HALF])
            if diagonal:
                at_u = lax.broadcasted_iota(jnp.int32, out.shape, 0)
                at_t = lax.broadcasted_iota(jnp.int32, out.shape, 1) + i * HALF
                out = jnp.where(at_u <= at_t, out, FAR_BELOW)
            return out

        found = {n: scores(n) for n in range(min(2, len(todo)))}
        ready = None
        for n in range(len(todo) + 1):
            now = None
            if n + 2 < len(todo):
                found[n + 2] = scores(n + 2)
            if n < len(todo):
                b, h, i = todo[n]
                cols = slice(i * HALF, i * HALF + HALF)
                score = found.pop(n)
                high = jnp.max(score, axis=0, keepdims=True)
                if diagonal:
                    peak, shrink = high, None
                else:
                    before = top[h, 0:1, cols]
                    peak = jnp.maximum(before, high)
                    shrink = jnp.exp2(before - peak)
                now = (b, h, cols, jnp.exp2(score - peak).astype(BF), shrink)
                top[h, 0:1, cols] = peak
            if ready is not None:
                b, h, cols, weights, shrink = ready
                mixed = dot(jnp.concatenate([blocks[b][128:], ones], axis=0), weights)
                acc[h, :, cols] = mixed if diagonal else mixed + acc[h, :, cols] * shrink
            ready = now

    def own_part(heads):
        absorb([kvall.at[c, zy]], heads, True)

        def visit(j, carry):
            absorb([kvall.at[j % 2, j // 2]], heads)
            return carry

        lax.fori_loop(zh * 8, s, visit, 0)

    def low_part(heads):
        def visit(j, carry):
            absorb([kvall.at[0, j], kvall.at[1, j]], heads)
            return carry

        lax.fori_loop(0, zh * 4, visit, 0)

    def teacher(h):
        done = acc[h]
        out = (done[:128] / done[128:129]).T
        teacher_ref[:, h * 128 : h * 128 + 128] = out.astype(BF)

    w = gathers
    place(0)
    enter(["R", "L", "Z", "S", "G"], p)
    w[0].a()
    place(1)
    w[1].a()
    place(2)
    w[2].a()
    raw = dot_t(rate_w_ref[...], x_ref[...])
    for d in range(4):
        rawsend[d] = jnp.concatenate([raw[4 * d : 4 * d + 4], raw[4 * d : 4 * d + 4]], axis=0)
    for d in range(3):
        raw_tile(d).start()
    place(3)
    place(4)
    for core in range(2):
        for at in range(8):
            src = (at * 2 + core) * 128
            xp[core, :, at * 128 : at * 128 + 128] = x_ref[:, src : src + 128]
    pieces = decays()
    w[0].b()
    w[3].a()
    w[1].b()
    w[0].c()
    w[0].d()
    multiply(0)
    w[4].a()
    w[1].c()
    w[2].b()
    settle(0)
    kv.a()
    w[1].d()
    multiply(1)
    local_state(pieces)
    w[2].c()
    w[3].b()
    kv.b()
    chip_state()
    st.a()
    settle(1)
    inside(pieces, 0)
    w[2].d()
    multiply(2)
    kv.c()
    st.b()
    w[3].c()
    w[4].b()
    settle(2)
    inside(pieces, 1)
    st.c()
    kv.near()
    own_part([0])
    w[3].d()
    multiply(3)
    w[4].c()
    own_part([1])
    settle(3)
    inside(pieces, 2)
    w[4].d()
    st.d()
    st.near()
    own_part([2])
    multiply(4)
    kv.d()
    st.e()
    incoming = arriving()
    for h in range(3):
        student(pieces, incoming, h)
    kv.e()
    low_part([0])
    low_part([1])
    settle(4)
    inside(pieces, 3)
    student(pieces, incoming, 3)
    low_part([2])
    own_part([3])
    low_part([3])
    for h in range(LOCAL_HEADS):
        teacher(h)
    for n in range(CHUNKS):
        w[n].sent()
        for cp in tiles(n):
            cp.wait_send()
    for d in range(3):
        raw_tile(d).wait_send()
    kv.sent()
    st.sent()
    swap().wait_send()


def tables():
    half = HEAD_DIM // 2
    freq = ROPE_BASE ** (-2.0 * np.arange(half) / HEAD_DIM)
    freq = np.concatenate([freq, freq])
    near = np.arange(TOK)[:, None] * freq[None]
    base = (np.arange(16) * TOK)[:, None] * freq[None]
    return (
        np.stack([np.cos(near), np.sin(near)]).astype(np.float32),
        np.stack([np.cos(base), np.sin(base)]).astype(np.float32),
    )


def body(layer_input, attn_weight, rate_weight, rate_bias, decay_rate, skip_gain):
    vmem = pl.BlockSpec(memory_space=pltpu.VMEM)
    smem = pl.BlockSpec(memory_space=pltpu.SMEM)
    dma = pltpu.SemaphoreType.DMA
    near, base = tables()
    heads = (LOCAL_HEADS, TOK, HEAD_DIM)
    return pl.pallas_call(
        window_kernel,
        name="window",
        out_shape=(
            jax.ShapeDtypeStruct((TOK, 512), BF),
            jax.ShapeDtypeStruct((TOK, 512), BF),
        ),
        in_specs=[vmem] * 5 + [smem] * 3,
        out_specs=(vmem, vmem),
        scratch_shapes=[
            pltpu.VMEM((CHUNKS, 2, 8, 128, 512), BF),
            pltpu.VMEM((2, TOK, 1024), BF),
            pltpu.VMEM((2, 4, TOK, 128), F32),
            pltpu.VMEM((4, 4, TOK, 128), BF),
            pltpu.VMEM((4, 3, TOK, 128), BF),
            pltpu.VMEM((2, TOK, 256), BF),
            pltpu.VMEM((3, TOK, 256), BF),
            pltpu.VMEM((4, 8, TOK), F32),
            pltpu.VMEM((3, 8, TOK), F32),
            pltpu.VMEM((2, 8, 256, TOK), BF),
            pltpu.VMEM((2, 8, 272, 128), BF),
            pltpu.VMEM((2, 528, 128), BF),
            pltpu.VMEM(heads, BF),
            pltpu.VMEM(heads, BF),
            pltpu.VMEM((TOK, HEAD_DIM), BF),
            pltpu.VMEM((TOK, HEAD_DIM), BF),
            pltpu.VMEM((2, LOCAL_HEADS, HEAD_DIM, HEAD_DIM), F32),
            pltpu.VMEM(heads, F32),
            pltpu.VMEM((LOCAL_HEADS, 144, TOK), F32),
            pltpu.VMEM((LOCAL_HEADS, 8, TOK), F32),
            dma((CHUNKS, COPIES)),
            dma((CHUNKS, COPIES)),
            dma((CHUNKS + 1, 3)),
            dma((CHUNKS + 1, 3)),
            dma((2, COPIES)),
            dma((2, COPIES)),
            dma,
            dma,
        ],
        compiler_params=pltpu.CompilerParams(
            collective_id=0, has_side_effects=True, vmem_limit_bytes=58 * 2**20
        ),
    )(
        layer_input, attn_weight.reshape(128, 2560), rate_weight.T, jnp.asarray(near),
        jnp.asarray(base), rate_bias, decay_rate, skip_gain,
    )


def solution(mesh):
    placed = (
        P("seq", "grp"),
        P(("grp", "seq"), "mdl", None),
        P("grp", "mdl"),
        P(("mdl", "grp")),
        P(("mdl", "grp")),
        P(("mdl", "grp")),
    )
    return jax.shard_map(
        body,
        mesh=mesh,
        in_specs=placed,
        out_specs=(P("seq", ("mdl", "grp")), P("seq", ("mdl", "grp"))),
        check_vma=False,
    )
```

time: 157 us -> 144 us (0.917)
  Pallas kernels: 150 us -> 138 us
    pallas_call x2 -> x1, Pallas kernels: 150 us -> 138 us  [body(): pl.pallas_call(window_kernel, name='window', out_shape=(jax.ShapeDtypeStr...]
where the time goes in v2:
time: 144 us
  Pallas kernels  138 us (96%)
  local copies, waits for them, and re-layouts  5.74 us (4%)
    pallas_call x1, Pallas kernels, body(): pl.pallas_call(window_kernel, name='window', out_shape=(jax.ShapeDtypeStr...  138 us
    unnamed x3, local copies, waits for them, and re-layouts  5.74 us

profile of v2, /device:TPU:217, one launch (start us, length us, event | category | flops | bytes accessed | tf_op | source)
XLA Modules:
  0.0 144.1 jit_solution(15230630274654100946)
XLA Ops:
  0.6 2.0 %copy.10 = bf16[16,8,2,1280]{3,1,2,0:T(8,128)(2,1)} copy(bf16[16,8,2,1280]{3,2,1,0:T(2,128)(2,1)} %bitcast.4) | data formatting | bytes 1310720
  2.6 137.7 %window.1 = (bf16[512,512]{1,0:T(8,128)(2,1)}, bf16[512,512]{1,0:T(8,128)(2,1)}) custom-call(bf16[512,2048]{1,0:T(8,128)(2,1)} %x_ref.1, bf16[128,2560]{1,0:T(8,128)(2,1)} %bitcast.3, bf16[16,2048]{1,0:T(8,128)(2,1)} %bitcast.5, f32[2,512,128]{2,1,0:T(8,128)} %constant.4.clone.near_ref, f32[2,16,128]{2,1,0:T(8,128)} %constant.5.clone.base_ref, f32[4]{0:T(128)} %bias_ref.1, ...), custom_call_target="tpu_custom_call" | custom-call | tf_op jit(solution)/shard_map/window/pallas_call | solution.py:573
  140.4 1.9 %copy.13 = bf16[512,512]{1,0:T(8,128)(2,1)} copy(bf16[512,512]{1,0:T(8,128)(2,1)} %get-tuple-element.4) | data formatting | bytes 1048576
  142.2 1.9 %copy.14 = bf16[512,512]{1,0:T(8,128)(2,1)} copy(bf16[512,512]{1,0:T(8,128)(2,1)} %get-tuple-element.5) | data formatting | bytes 1048576

commit v3 on v2

--- a/solution.py
+++ b/solution.py
@@ -15,7 +15,7 @@
 FAR_BELOW = -1e30
 TOK = 512
 LOCAL_HEADS = 4
-CHUNKS = 5
+KINDS = ("k", "v", "q0", "q1", "q2", "q3")
 COPIES = 11
 HALF = 256
 SCALE = HEAD_DIM**-0.5
@@ -105,9 +105,11 @@
     def across(self, own):
         return self.copy(4, self.p["Z"], self.base(own) + self.p["y"])
 
-    def a(self):
+    def ay(self):
         for cp in self.spread(True):
             cp.start()
+
+    def az(self):
         self.across(True).start()
 
     def pass_on(self, own):
@@ -115,8 +117,10 @@
             got.wait_recv()
             on.start()
 
-    def b(self):
+    def f(self):
         self.pass_on(True)
+
+    def zs(self):
         self.across(False).wait_recv()
         for cp in self.spread(False):
             cp.start()
@@ -126,11 +130,13 @@
             cp.wait_recv()
         self.four(9 if own else 10, own, self.p["c"]).start()
 
-    def c(self):
+    def s1(self):
         self.finish(True)
+
+    def zf(self):
         self.pass_on(False)
 
-    def d(self):
+    def s2(self):
         self.finish(False)
 
     def e(self):
@@ -214,21 +220,32 @@
 def window_kernel(
     x_ref, w_ref, rate_w_ref, near_ref, base_ref, bias_ref, rate_ref, skip_ref,
     teacher_ref, student_ref,
-    wg, xp, own, qsend, qrecv, kvsend, kvrecv, rawsend, rawrecv,
-    kvall, stall, sx, rq, ct, vrow, brow, contrib, inner, acc, top,
+    wkv, wq, xp, own_kv, own_q, qsend, qrecv, kvsend, kvrecv, rawsend, rawrecv,
+    kall, vall, stall, sx, rq, ct, vrow, brow, contrib, inner, acc, top,
     wssem, wrsem, gssem, grsem, kssem, krsem, xssem, xrsem,
 ):
     p = places()
     g, s, zh, c, zy = p["g"], p["s"], p["zh"], p["c"], p["zy"]
-    gathers = [Gather(wg.at[n], wssem.at[n], wrsem.at[n], p, 64) for n in range(CHUNKS)]
-    kv = Earlier(kvall, kssem.at[0], krsem.at[0], p, 128)
-    st = Earlier(stall, kssem.at[1], krsem.at[1], p, 128)
-
-    def place(chunk):
+    w = {}
+    for n, name in enumerate(KINDS):
+        buf = wkv.at[n] if n < 2 else wq.at[n - 2]
+        w[name] = Gather(buf, wssem.at[n], wrsem.at[n], p, 64)
+    kept = {
+        name: Earlier(buf, kssem.at[n], krsem.at[n], p, half)
+        for n, (name, buf, half) in enumerate((("k", kall, 64), ("v", vall, 64), ("s", stall, 128)))
+    }
+
+    def place(name):
+        if name in "kv":
+            n = "kv".index(name)
+            for k in range(2):
+                first = k * 1280 + 1024 + n * 128
+                wkv[n, c, zy, :, k * 128 : k * 128 + 128] = w_ref[:, first : first + 128]
+            return
+        n = int(name[1])
         for d in range(4):
-            k = d // 2
-            first = k * 1280 + (1024 + (d % 2) * 128 if chunk == 0 else (d % 2) * 512 + (chunk - 1) * 128)
-            wg[chunk, c, zy, :, d * 128 : d * 128 + 128] = w_ref[:, first : first + 128]
+            first = d // 2 * 1280 + d % 2 * 512 + n * 128
+            wq[n, c, zy, :, d * 128 : d * 128 + 128] = w_ref[:, first : first + 128]
 
     def tile(source, target, k, d):
         return pltpu.make_async_remote_copy(
@@ -237,12 +254,30 @@
         )
 
     def raw_tile(d):
-        return tile(rawsend.at[lax.rem(g + d + 1, 4)], rawrecv.at[d], CHUNKS, d)
-
-    def tiles(n):
-        if n == 0:
-            return [tile(kvsend.at[lax.rem(g + d + 1, 4) // 2], kvrecv.at[d], 0, d) for d in range(3)]
-        return [tile(qsend.at[n - 1, lax.rem(g + d + 1, 4)], qrecv.at[n - 1, d], n, d) for d in range(3)]
+        return tile(rawsend.at[lax.rem(g + d + 1, 4)], rawrecv.at[d], len(KINDS), d)
+
+    def tiles(name):
+        k = KINDS.index(name)
+        if k < 2:
+            return [
+                tile(kvsend.at[k, lax.rem(g + d + 1, 4) // 2], kvrecv.at[k, d], k, d) for d in range(3)
+            ]
+        return [
+            tile(qsend.at[k - 2, lax.rem(g + d + 1, 4)], qrecv.at[k - 2, d], k, d) for d in range(3)
+        ]
+
+    def send_raw():
+        raw = dot_t(rate_w_ref[...], x_ref[...])
+        for d in range(4):
+            rawsend[d] = jnp.concatenate([raw[4 * d : 4 * d + 4], raw[4 * d : 4 * d + 4]], axis=0)
+        for d in range(3):
+            raw_tile(d).start()
+
+    def arrange():
+        for core in range(2):
+            for at in range(8):
+                src = (at * 2 + core) * 128
+                xp[core, :, at * 128 : at * 128 + 128] = x_ref[:, src : src + 128]
 
     def rotate(u):
         near_c, near_s = near_ref[0], near_ref[1]
@@ -253,40 +288,40 @@
         sine = (near_s * far_c + near_c * far_s) * sign
         return u * cosine + pltpu.roll(u, HEAD_DIM // 2, 1) * sine
 
-    def multiply(n):
-        gathers[n].e()
-        out = sum(dot(xp[core], wg[n, core].reshape(1024, 512)) for core in range(2))
-        for d in range(4):
+    def multiply(name):
+        w[name].e()
+        k = KINDS.index(name)
+        buf = wkv.at[k] if k < 2 else wq.at[k - 2]
+        out = sum(dot(xp[core], buf[core].reshape(1024, buf.shape[-1])) for core in range(2))
+        for d in range(buf.shape[-1] // 128):
             part = out[:, d * 128 : d * 128 + 128]
-            own[n % 2, d] = part
-            if n == 0:
-                kvsend[d // 2, :, (d % 2) * 128 : (d % 2) * 128 + 128] = part.astype(BF)
+            if k < 2:
+                own_kv[k, d] = part
+                kvsend[k, d] = part.astype(BF)
             else:
-                qsend[n - 1, d] = part.astype(BF)
-        for cp in tiles(n):
+                own_q[k % 2, d] = part
+                qsend[k - 2, d] = part.astype(BF)
+        for cp in tiles(name):
             cp.start()
 
-    def settle(n):
-        for cp in tiles(n):
+    def settle(name):
+        k = KINDS.index(name)
+        for cp in tiles(name):
             cp.wait_recv()
-        if n == 0:
-            k = g // 2
-            keys, value = own[0, 2 * k], own[0, 2 * k + 1]
-            for d in range(3):
-                keys = keys + kvrecv[d, :, :128].astype(F32)
-                value = value + kvrecv[d, :, 128:].astype(F32)
-            turned = rotate(keys).astype(BF)
+        got = own_kv[k, g // 2] if k < 2 else own_q[k % 2, g]
+        for d in range(3):
+            got = got + (kvrecv[k, d] if k < 2 else qrecv[k - 2, d]).astype(F32)
+        if name == "k":
+            turned = rotate(got).astype(BF)
             for i in range(4):
-                kvall[c, zy, :128, i * 128 : i * 128 + 128] = turned[i * 128 : i * 128 + 128]
-            kvall[c, zy, 128:] = value.T.astype(BF)
-            vrow[...] = value.astype(BF)
-            brow[...] = keys.astype(BF)
+                kall[c, zy, :, i * 128 : i * 128 + 128] = turned[i * 128 : i * 128 + 128]
+            brow[...] = got.astype(BF)
+        elif name == "v":
+            vall[c, zy] = got.T.astype(BF)
+            vrow[...] = got.astype(BF)
         else:
-            query = own[n % 2, g]
-            for d in range(3):
-                query = query + qrecv[n - 1, d].astype(F32)
-            ct[n - 1] = query.astype(BF)
-            rq[n - 1] = (rotate(query) * (SCALE * LOG2E)).astype(BF)
+            ct[k - 2] = got.astype(BF)
+            rq[k - 2] = (rotate(got) * (SCALE * LOG2E)).astype(BF)
 
     row = lax.broadcasted_iota(jnp.int32, (8, TOK), 0)
 
@@ -408,7 +443,8 @@
 
         def scores(n):
             b, h, i = todo[n]
-            keys = jnp.concatenate([blocks[b][:128, k * 128 : k * 128 + 128] for k in range(4)], axis=0)
+            keys = kall[(*blocks[b],)]
+            keys = jnp.concatenate([keys[:, k * 128 : k * 128 + 128] for k in range(4)], axis=0)
             out = dot_t(keys, rq[h, i * HALF : i * HALF + HALF])
             if diagonal:
                 at_u = lax.broadcasted_iota(jnp.int32, out.shape, 0)
@@ -437,118 +473,156 @@
                 top[h, 0:1, cols] = peak
             if ready is not None:
                 b, h, cols, weights, shrink = ready
-                mixed = dot(jnp.concatenate([blocks[b][128:], ones], axis=0), weights)
+                mixed = dot(jnp.concatenate([vall[(*blocks[b],)], ones], axis=0), weights)
                 acc[h, :, cols] = mixed if diagonal else mixed + acc[h, :, cols] * shrink
             ready = now
 
-    def own_part(heads):
-        absorb([kvall.at[c, zy]], heads, True)
+    def own_part(heads, part):
+        if part == 0:
+            absorb([(c, zy)], heads, True)
+            pl.when(c == 1)(lambda: absorb([(0, zy)], heads))
+            return
 
         def visit(j, carry):
-            absorb([kvall.at[j % 2, j // 2]], heads)
+            absorb([(0, j), (1, j)], heads)
             return carry
 
-        lax.fori_loop(zh * 8, s, visit, 0)
-
-    def low_part(heads):
-        def visit(j, carry):
-            absorb([kvall.at[0, j], kvall.at[1, j]], heads)
-            return carry
-
-        lax.fori_loop(0, zh * 4, visit, 0)
+        lax.fori_loop(zh * 4, zy, visit, 0)
+
+    def low_part(heads, part):
+        first = part * 2
+
+        def both():
+            if len(heads) > 1:
+                absorb([(0, first), (1, first)], heads)
+                absorb([(0, first + 1), (1, first + 1)], heads)
+            else:
+                absorb([(k % 2, first + k // 2) for k in range(4)], heads)
+
+        pl.when(zh == 1)(both)
 
     def teacher(h):
         done = acc[h]
         out = (done[:128] / done[128:129]).T
         teacher_ref[:, h * 128 : h * 128 + 128] = out.astype(BF)
 
-    w = gathers
-    place(0)
+    place("k")
     enter(["R", "L", "Z", "S", "G"], p)
-    w[0].a()
-    place(1)
-    w[1].a()
-    place(2)
-    w[2].a()
-    raw = dot_t(rate_w_ref[...], x_ref[...])
-    for d in range(4):
-        rawsend[d] = jnp.concatenate([raw[4 * d : 4 * d + 4], raw[4 * d : 4 * d + 4]], axis=0)
-    for d in range(3):
-        raw_tile(d).start()
-    place(3)
-    place(4)
-    for core in range(2):
-        for at in range(8):
-            src = (at * 2 + core) * 128
-            xp[core, :, at * 128 : at * 128 + 128] = x_ref[:, src : src + 128]
+    w["k"].ay()
+    place("v")
+    w["v"].az()
+    w["v"].ay()
+    place("q3")
+    send_raw()
+    place("q0")
+    w["q0"].ay()
+    w["k"].az()
+    place("q1")
+    place("q2")
+    w["q1"].az()
+    w["q1"].ay()
+    w["q0"].az()
+    w["q3"].az()
+    w["v"].zs()
     pieces = decays()
-    w[0].b()
-    w[3].a()
-    w[1].b()
-    w[0].c()
-    w[0].d()
-    multiply(0)
-    w[4].a()
-    w[1].c()
-    w[2].b()
-    settle(0)
-    kv.a()
-    w[1].d()
-    multiply(1)
+    w["k"].zs()
+    w["v"].f()
+    w["v"].zf()
+    w["k"].f()
+    w["k"].zf()
+    w["q1"].f()
+    w["q2"].az()
+    w["v"].s1()
+    w["v"].s2()
+    w["q0"].f()
+    w["q1"].zs()
+    w["k"].s1()
+    arrange()
+    w["k"].s2()
+    w["q3"].ay()
+    multiply("v")
+    w["q1"].s1()
+    multiply("k")
+    w["q0"].s1()
+    w["q1"].zf()
+    w["q0"].zs()
+    w["q1"].s2()
+    settle("v")
+    kept["v"].a()
+    w["q0"].zf()
+    multiply("q1")
+    w["q3"].zs()
+    settle("k")
+    kept["v"].b()
+    w["q0"].s2()
     local_state(pieces)
-    w[2].c()
-    w[3].b()
-    kv.b()
+    kept["k"].a()
+    multiply("q0")
+    w["q3"].f()
+    kept["v"].c()
+    w["q3"].zf()
+    kept["k"].b()
+    kept["v"].near()
+    w["q3"].s1()
+    w["q2"].ay()
+    w["q2"].zs()
+    w["q3"].s2()
+    settle("q1")
+    inside(pieces, 1)
+    kept["k"].c()
     chip_state()
-    st.a()
-    settle(1)
+    kept["s"].a()
+    settle("q0")
     inside(pieces, 0)
-    w[2].d()
-    multiply(2)
-    kv.c()
-    st.b()
-    w[3].c()
-    w[4].b()
-    settle(2)
-    inside(pieces, 1)
-    st.c()
-    kv.near()
-    own_part([0])
-    w[3].d()
-    multiply(3)
-    w[4].c()
-    own_part([1])
-    settle(3)
+    multiply("q3")
+    kept["k"].near()
+    own_part([0, 1], 0)
+    kept["v"].d()
+    w["q2"].f()
+    w["q2"].zf()
+    own_part([0, 1], 1)
+    w["q2"].s2()
+    w["q2"].s1()
+    kept["s"].b()
+    kept["v"].e()
+    settle("q3")
+    own_part([3], 0)
+    inside(pieces, 3)
+    kept["k"].d()
+    own_part([3], 1)
+    kept["s"].c()
+    multiply("q2")
+    kept["k"].e()
+    low_part([0, 1], 0)
+    kept["s"].d()
+    low_part([0, 1], 1)
+    teacher(1)
+    low_part([3], 0)
+    low_part([3], 1)
+    settle("q2")
     inside(pieces, 2)
-    w[4].d()
-    st.d()
-    st.near()
-    own_part([2])
-    multiply(4)
-    kv.d()
-    st.e()
+    kept["s"].e()
+    own_part([2], 0)
+    low_part([2], 1)
+    kept["s"].near()
+    own_part([2], 1)
     incoming = arriving()
-    for h in range(3):
-        student(pieces, incoming, h)
-    kv.e()
-    low_part([0])
-    low_part([1])
-    settle(4)
-    inside(pieces, 3)
+    student(pieces, incoming, 1)
+    student(pieces, incoming, 0)
+    teacher(0)
     student(pieces, incoming, 3)
-    low_part([2])
-    own_part([3])
-    low_part([3])
-    for h in range(LOCAL_HEADS):
-        teacher(h)
-    for n in range(CHUNKS):
-        w[n].sent()
-        for cp in tiles(n):
+    low_part([2], 0)
+    teacher(2)
+    teacher(3)
+    student(pieces, incoming, 2)
+    for name in KINDS:
+        w[name].sent()
+        for cp in tiles(name):
             cp.wait_send()
     for d in range(3):
         raw_tile(d).wait_send()
-    kv.sent()
-    st.sent()
+    for name in kept:
+        kept[name].sent()
     swap().wait_send()
 
 
@@ -580,16 +654,19 @@
         in_specs=[vmem] * 5 + [smem] * 3,
         out_specs=(vmem, vmem),
         scratch_shapes=[
-            pltpu.VMEM((CHUNKS, 2, 8, 128, 512), BF),
+            pltpu.VMEM((2, 2, 8, 128, 256), BF),
+            pltpu.VMEM((4, 2, 8, 128, 512), BF),
             pltpu.VMEM((2, TOK, 1024), BF),
+            pltpu.VMEM((2, 2, TOK, 128), F32),
             pltpu.VMEM((2, 4, TOK, 128), F32),
             pltpu.VMEM((4, 4, TOK, 128), BF),
             pltpu.VMEM((4, 3, TOK, 128), BF),
-            pltpu.VMEM((2, TOK, 256), BF),
-            pltpu.VMEM((3, TOK, 256), BF),
+            pltpu.VMEM((2, 2, TOK, 128), BF),
+            pltpu.VMEM((2, 3, TOK, 128), BF),
             pltpu.VMEM((4, 8, TOK), F32),
             pltpu.VMEM((3, 8, TOK), F32),
-            pltpu.VMEM((2, 8, 256, TOK), BF),
+            pltpu.VMEM((2, 8, 128, TOK), BF),
+            pltpu.VMEM((2, 8, 128, TOK), BF),
             pltpu.VMEM((2, 8, 272, 128), BF),
             pltpu.VMEM((2, 528, 128), BF),
             pltpu.VMEM(heads, BF),
@@ -600,12 +677,12 @@
             pltpu.VMEM(heads, F32),
             pltpu.VMEM((LOCAL_HEADS, 144, TOK), F32),
             pltpu.VMEM((LOCAL_HEADS, 8, TOK), F32),
-            dma((CHUNKS, COPIES)),
-            dma((CHUNKS, COPIES)),
-            dma((CHUNKS + 1, 3)),
-            dma((CHUNKS + 1, 3)),
-            dma((2, COPIES)),
-            dma((2, COPIES)),
+            dma((len(KINDS), COPIES)),
+            dma((len(KINDS), COPIES)),
+            dma((len(KINDS) + 1, 3)),
+            dma((len(KINDS) + 1, 3)),
+            dma((3, COPIES)),
+            dma((3, COPIES)),
             dma,
             dma,
         ],

time: 144 us -> 120 us (0.83)
  Pallas kernels: 138 us -> 113 us
    pallas_call x1, Pallas kernels: 138 us -> 113 us  [body(): pl.pallas_call(window_kernel, name='window', out_shape=(jax.ShapeDtypeStr...]
where the time goes in v3:
time: 120 us; the launch traced here: 119 us
  Pallas kernels  113 us (94%)
  local copies, waits for them, and re-layouts  5.74 us (5%)
    pallas_call x1, Pallas kernels, body(): pl.pallas_call(window_kernel, name='window', out_shape=(jax.ShapeDtypeStr...  113 us
    unnamed x3, local copies, waits for them, and re-layouts  5.74 us

profile of v3, /device:TPU:217, one launch (start us, length us, event | category | flops | bytes accessed | tf_op | source)
XLA Modules:
  0.0 119.4 jit_solution(16394576092496688263)
XLA Ops:
  0.6 2.0 %copy.10 = bf16[16,8,2,1280]{3,1,2,0:T(8,128)(2,1)} copy(bf16[16,8,2,1280]{3,2,1,0:T(2,128)(2,1)} %bitcast.4) | data formatting | bytes 1310720
  2.6 113.0 %window.1 = (bf16[512,512]{1,0:T(8,128)(2,1)}, bf16[512,512]{1,0:T(8,128)(2,1)}) custom-call(bf16[512,2048]{1,0:T(8,128)(2,1)} %x_ref.1, bf16[128,2560]{1,0:T(8,128)(2,1)} %bitcast.3, bf16[16,2048]{1,0:T(8,128)(2,1)} %bitcast.5, f32[2,512,128]{2,1,0:T(8,128)} %constant.4.clone.near_ref, f32[2,16,128]{2,1,0:T(8,128)} %constant.5.clone.base_ref, f32[4]{0:T(128)} %bias_ref.1, ...), custom_call_target="tpu_custom_call" | custom-call | tf_op jit(solution)/shard_map/window/pallas_call | solution.py:647
  115.7 1.9 %copy.13 = bf16[512,512]{1,0:T(8,128)(2,1)} copy(bf16[512,512]{1,0:T(8,128)(2,1)} %get-tuple-element.4) | data formatting | bytes 1048576
  117.5 1.9 %copy.14 = bf16[512,512]{1,0:T(8,128)(2,1)} copy(bf16[512,512]{1,0:T(8,128)(2,1)} %get-tuple-element.5) | data formatting | bytes 1048576

commit v4 on v3

--- a/solution.py
+++ b/solution.py
@@ -152,10 +152,6 @@
 
 
 class Earlier(Gather):
-    def lift(self, n):
-        at = [self.p["y"], self.p["down"], self.p["up"], self.p["far"]][n]
-        return self.copy(4 + n, self.p["Z"], at)
-
     def low(self, f):
         pl.when(self.p["zh"] == 0)(f)
 
@@ -163,33 +159,26 @@
         pl.when(self.p["zh"] == 1)(f)
 
     def a(self):
-        for cp in self.spread(True):
-            cp.start()
-        self.low(lambda: self.lift(0).start())
+        self.low(self.az)
+        self.ay()
 
     def b(self):
-        self.pass_on(True)
-
-        def send():
-            self.lift(1).start()
-            self.lift(2).start()
-
-        self.low(send)
+        self.f()
 
     def c(self):
-        self.finish(True)
-        self.low(lambda: self.lift(3).start())
+        self.s1()
 
     def near(self):
         self.four(9, True, 1 - self.p["c"]).wait_recv()
 
+    def zs(self):
+        self.high(super().zs)
+
+    def zf(self):
+        self.high(super().zf)
+
     def d(self):
-        def hand():
-            for n in range(4):
-                self.lift(n).wait_recv()
-            self.four(10, False, self.p["c"]).start()
-
-        self.high(hand)
+        self.high(self.s2)
 
     def e(self):
         self.high(lambda: self.four(10, False, 1 - self.p["c"]).wait_recv())
@@ -198,13 +187,14 @@
         for cp in (*self.spread(True), *self.forward(True)):
             cp.wait_send()
         self.four(9, True, self.p["c"]).wait_send()
-
-        def lifted():
-            for n in range(4):
-                self.lift(n).wait_send()
-
-        self.low(lifted)
-        self.high(lambda: self.four(10, False, self.p["c"]).wait_send())
+        self.low(lambda: self.across(True).wait_send())
+
+        def other():
+            for cp in (*self.spread(False), *self.forward(False)):
+                cp.wait_send()
+            self.four(10, False, self.p["c"]).wait_send()
+
+        self.high(other)
 
 
 def dot(a, b):
@@ -509,111 +499,117 @@
     place("k")
     enter(["R", "L", "Z", "S", "G"], p)
     w["k"].ay()
+    w["k"].az()
     place("v")
-    w["v"].az()
     w["v"].ay()
-    place("q3")
-    send_raw()
     place("q0")
     w["q0"].ay()
-    w["k"].az()
+    send_raw()
     place("q1")
-    place("q2")
-    w["q1"].az()
-    w["q1"].ay()
-    w["q0"].az()
-    w["q3"].az()
-    w["v"].zs()
+    w["v"].az()
+    w["k"].f()
+    w["v"].f()
     pieces = decays()
     w["k"].zs()
-    w["v"].f()
+    w["q0"].az()
+    w["q1"].ay()
+    place("q2")
+    w["v"].zs()
+    w["q1"].az()
+    w["k"].s1()
+    w["q0"].f()
+    w["v"].s1()
+    w["k"].zf()
     w["v"].zf()
-    w["k"].f()
-    w["k"].zf()
     w["q1"].f()
+    w["q2"].ay()
+    w["q0"].zs()
+    place("q3")
     w["q2"].az()
-    w["v"].s1()
+    w["k"].s2()
     w["v"].s2()
-    w["q0"].f()
+    w["q1"].s1()
+    arrange()
+    multiply("v")
+    w["q2"].f()
     w["q1"].zs()
-    w["k"].s1()
-    arrange()
-    w["k"].s2()
-    w["q3"].ay()
-    multiply("v")
-    w["q1"].s1()
+    w["q3"].az()
+    w["q0"].zf()
+    w["q0"].s1()
     multiply("k")
-    w["q0"].s1()
+    w["q2"].s1()
+    w["q2"].zs()
     w["q1"].zf()
-    w["q0"].zs()
-    w["q1"].s2()
     settle("v")
     kept["v"].a()
-    w["q0"].zf()
+    w["q0"].s2()
+    multiply("q0")
+    w["q2"].zf()
+    w["q1"].s2()
+    settle("k")
+    kept["k"].a()
+    local_state(pieces)
+    chip_state()
+    w["q2"].s2()
+    kept["v"].b()
+    w["q3"].ay()
     multiply("q1")
+    kept["k"].b()
+    settle("q0")
+    multiply("q2")
     w["q3"].zs()
-    settle("k")
-    kept["v"].b()
-    w["q0"].s2()
-    local_state(pieces)
-    kept["k"].a()
-    multiply("q0")
+    kept["v"].c()
+    kept["v"].zs()
+    inside(pieces, 0)
     w["q3"].f()
-    kept["v"].c()
-    w["q3"].zf()
-    kept["k"].b()
-    kept["v"].near()
-    w["q3"].s1()
-    w["q2"].ay()
-    w["q2"].zs()
-    w["q3"].s2()
+    kept["k"].c()
+    kept["k"].zs()
     settle("q1")
     inside(pieces, 1)
-    kept["k"].c()
-    chip_state()
+    kept["k"].near()
+    kept["v"].near()
+    w["q3"].zf()
+    own_part([0, 1], 0)
+    kept["v"].zf()
+    own_part([0, 1], 1)
+    kept["k"].zf()
     kept["s"].a()
-    settle("q0")
-    inside(pieces, 0)
+    settle("q2")
+    w["q3"].s1()
+    own_part([2], 0)
+    w["q3"].s2()
+    kept["v"].d()
+    own_part([2], 1)
+    kept["k"].d()
+    kept["s"].b()
+    inside(pieces, 2)
+    kept["v"].e()
+    kept["s"].zs()
     multiply("q3")
-    kept["k"].near()
-    own_part([0, 1], 0)
-    kept["v"].d()
-    w["q2"].f()
-    w["q2"].zf()
-    own_part([0, 1], 1)
-    w["q2"].s2()
-    w["q2"].s1()
-    kept["s"].b()
-    kept["v"].e()
+    kept["k"].e()
+    low_part([2], 0)
+    kept["s"].zf()
+    kept["s"].c()
+    low_part([0, 1], 1)
+    kept["s"].d()
+    low_part([0, 1], 0)
     settle("q3")
     own_part([3], 0)
-    inside(pieces, 3)
-    kept["k"].d()
+    low_part([3], 1)
+    low_part([3], 0)
     own_part([3], 1)
-    kept["s"].c()
-    multiply("q2")
-    kept["k"].e()
-    low_part([0, 1], 0)
-    kept["s"].d()
-    low_part([0, 1], 1)
-    teacher(1)
-    low_part([3], 0)
-    low_part([3], 1)
-    settle("q2")
-    inside(pieces, 2)
     kept["s"].e()
-    own_part([2], 0)
     low_part([2], 1)
+    teacher(2)
     kept["s"].near()
-    own_part([2], 1)
     incoming = arriving()
     student(pieces, incoming, 1)
+    teacher(1)
+    inside(pieces, 3)
+    student(pieces, incoming, 3)
+    teacher(3)
     student(pieces, incoming, 0)
     teacher(0)
-    student(pieces, incoming, 3)
-    low_part([2], 0)
-    teacher(2)
-    teacher(3)
     student(pieces, incoming, 2)
     for name in KINDS:
         w[name].sent()

time: 120 us -> 99.3 us (0.83)
  Pallas kernels: 113 us -> 92.2 us
    pallas_call x1, Pallas kernels: 113 us -> 92.2 us  [body(): pl.pallas_call(window_kernel, name='window', out_shape=(jax.ShapeDtypeStr...]
where the time goes in v4:
time: 99.3 us; the launch traced here: 98.5 us
  Pallas kernels  92.2 us (93%)
  local copies, waits for them, and re-layouts  5.74 us (6%)
    pallas_call x1, Pallas kernels, body(): pl.pallas_call(window_kernel, name='window', out_shape=(jax.ShapeDtypeStr...  92.2 us
    unnamed x3, local copies, waits for them, and re-layouts  5.74 us

profile of v4, /device:TPU:217, one launch (start us, length us, event | category | flops | bytes accessed | tf_op | source)
XLA Modules:
  0.0 98.5 jit_solution(15359445269470558237)
XLA Ops:
  0.6 2.0 %copy.10 = bf16[16,8,2,1280]{3,1,2,0:T(8,128)(2,1)} copy(bf16[16,8,2,1280]{3,2,1,0:T(2,128)(2,1)} %bitcast.4) | data formatting | bytes 1310720
  2.6 92.2 %window.1 = (bf16[512,512]{1,0:T(8,128)(2,1)}, bf16[512,512]{1,0:T(8,128)(2,1)}) custom-call(bf16[512,2048]{1,0:T(8,128)(2,1)} %x_ref.1, bf16[128,2560]{1,0:T(8,128)(2,1)} %bitcast.3, bf16[16,2048]{1,0:T(8,128)(2,1)} %bitcast.5, f32[2,512,128]{2,1,0:T(8,128)} %constant.4.clone.near_ref, f32[2,16,128]{2,1,0:T(8,128)} %constant.5.clone.base_ref, f32[4]{0:T(128)} %bias_ref.1, ...), custom_call_target="tpu_custom_call" | custom-call | tf_op jit(solution)/shard_map/window/pallas_call | solution.py:643
  94.8 1.9 %copy.13 = bf16[512,512]{1,0:T(8,128)(2,1)} copy(bf16[512,512]{1,0:T(8,128)(2,1)} %get-tuple-element.4) | data formatting | bytes 1048576
  96.7 1.9 %copy.14 = bf16[512,512]{1,0:T(8,128)(2,1)} copy(bf16[512,512]{1,0:T(8,128)(2,1)} %get-tuple-element.5) | data formatting | bytes 1048576

commit v5 on v4

--- a/solution.py
+++ b/solution.py
@@ -212,7 +212,7 @@
     teacher_ref, student_ref,
     wkv, wq, xp, own_kv, own_q, qsend, qrecv, kvsend, kvrecv, rawsend, rawrecv,
     kall, vall, stall, sx, rq, ct, vrow, brow, contrib, inner, acc, top,
-    wssem, wrsem, gssem, grsem, kssem, krsem, xssem, xrsem,
+    wssem, wrsem, gssem, grsem, kssem, krsem, xssem, xrsem, xsem,
 ):
     p = places()
     g, s, zh, c, zy = p["g"], p["s"], p["zh"], p["c"], p["zy"]
@@ -229,13 +229,13 @@
         if name in "kv":
             n = "kv".index(name)
             for k in range(2):
-                first = k * 1280 + 1024 + n * 128
-                wkv[n, c, zy, :, k * 128 : k * 128 + 128] = w_ref[:, first : first + 128]
+                first = 1024 + n * 128
+                wkv[n, c, zy, :, k * 128 : k * 128 + 128] = w_ref[:, k, first : first + 128]
             return
         n = int(name[1])
         for d in range(4):
-            first = d // 2 * 1280 + d % 2 * 512 + n * 128
-            wq[n, c, zy, :, d * 128 : d * 128 + 128] = w_ref[:, first : first + 128]
+            first = d % 2 * 512 + n * 128
+            wq[n, c, zy, :, d * 128 : d * 128 + 128] = w_ref[:, d // 2, first : first + 128]
 
     def tile(source, target, k, d):
         return pltpu.make_async_remote_copy(
@@ -256,18 +256,28 @@
             tile(qsend.at[k - 2, lax.rem(g + d + 1, 4)], qrecv.at[k - 2, d], k, d) for d in range(3)
         ]
 
+    def x_copies():
+        for core in range(2):
+            for at in range(8):
+                src = (at * 2 + core) * 128
+                yield pltpu.make_async_copy(
+                    x_ref.at[:, src : src + 128], xp.at[core, :, at * 128 : at * 128 + 128],
+                    xsem.at[core * 8 + at],
+                )
+
+    def arrange():
+        for cp in x_copies():
+            cp.wait()
+
     def send_raw():
-        raw = dot_t(rate_w_ref[...], x_ref[...])
+        raw = 0.0
+        for core in range(2):
+            parts = [rate_w_ref[:, (at * 2 + core) * 128 : (at * 2 + core) * 128 + 128] for at in range(8)]
+            raw = raw + dot_t(jnp.concatenate(parts, axis=1), xp[core])
         for d in range(4):
             rawsend[d] = jnp.concatenate([raw[4 * d : 4 * d + 4], raw[4 * d : 4 * d + 4]], axis=0)
         for d in range(3):
             raw_tile(d).start()
-
-    def arrange():
-        for core in range(2):
-            for at in range(8):
-                src = (at * 2 + core) * 128
-                xp[core, :, at * 128 : at * 128 + 128] = x_ref[:, src : src + 128]
 
     def rotate(u):
         near_c, near_s = near_ref[0], near_ref[1]
@@ -470,6 +480,8 @@
     def own_part(heads, part):
         if part == 0:
             absorb([(c, zy)], heads, True)
+            return
+        if part == 1:
             pl.when(c == 1)(lambda: absorb([(0, zy)], heads))
             return
 
@@ -496,121 +508,126 @@
         out = (done[:128] / done[128:129]).T
         teacher_ref[:, h * 128 : h * 128 + 128] = out.astype(BF)
 
+    for cp in x_copies():
+        cp.start()
     place("k")
     enter(["R", "L", "Z", "S", "G"], p)
     w["k"].ay()
     w["k"].az()
+    arrange()
+    send_raw()
     place("v")
     w["v"].ay()
     place("q0")
     w["q0"].ay()
-    send_raw()
-    place("q1")
+    w["k"].f()
+    place("q3")
     w["v"].az()
-    w["k"].f()
     w["v"].f()
-    pieces = decays()
+    w["q3"].ay()
     w["k"].zs()
     w["q0"].az()
-    w["q1"].ay()
-    place("q2")
-    w["v"].zs()
-    w["q1"].az()
     w["k"].s1()
     w["q0"].f()
     w["v"].s1()
+    w["v"].zs()
     w["k"].zf()
+    w["q3"].f()
+    place("q1")
+    w["q1"].ay()
+    w["q1"].az()
+    w["q0"].s1()
     w["v"].zf()
+    w["k"].s2()
+    w["q3"].s1()
+    place("q2")
+    w["q0"].zs()
+    w["q2"].az()
+    w["q2"].ay()
+    multiply("k")
+    pieces = decays()
+    w["v"].s2()
+    w["q0"].zf()
+    w["q1"].zs()
+    w["q3"].az()
     w["q1"].f()
-    w["q2"].ay()
-    w["q0"].zs()
-    place("q3")
-    w["q2"].az()
-    w["k"].s2()
-    w["v"].s2()
-    w["q1"].s1()
-    arrange()
     multiply("v")
     w["q2"].f()
-    w["q1"].zs()
-    w["q3"].az()
-    w["q0"].zf()
-    w["q0"].s1()
-    multiply("k")
-    w["q2"].s1()
+    w["q0"].s2()
+    w["q1"].zf()
     w["q2"].zs()
-    w["q1"].zf()
-    settle("v")
-    kept["v"].a()
-    w["q0"].s2()
-    multiply("q0")
-    w["q2"].zf()
-    w["q1"].s2()
+    w["q1"].s1()
     settle("k")
     kept["k"].a()
+    multiply("q0")
+    w["q2"].s1()
+    w["q1"].s2()
+    settle("v")
     local_state(pieces)
-    chip_state()
+    w["q2"].zf()
+    w["q3"].zs()
+    kept["v"].a()
+    multiply("q1")
     w["q2"].s2()
-    kept["v"].b()
-    w["q3"].ay()
-    multiply("q1")
+    w["q3"].zf()
     kept["k"].b()
     settle("q0")
     multiply("q2")
-    w["q3"].zs()
-    kept["v"].c()
+    kept["v"].b()
+    kept["k"].zs()
+    chip_state()
+    kept["s"].a()
     kept["v"].zs()
     inside(pieces, 0)
-    w["q3"].f()
+    w["q3"].s2()
     kept["k"].c()
-    kept["k"].zs()
+    kept["v"].c()
     settle("q1")
+    own_part([0, 1], 0)
+    multiply("q3")
+    kept["k"].near()
+    kept["s"].zs()
     inside(pieces, 1)
-    kept["k"].near()
+    kept["k"].zf()
     kept["v"].near()
-    w["q3"].zf()
-    own_part([0, 1], 0)
+    own_part([0, 1], 2)
     kept["v"].zf()
-    own_part([0, 1], 1)
-    kept["k"].zf()
-    kept["s"].a()
+    kept["s"].b()
     settle("q2")
-    w["q3"].s1()
+    inside(pieces, 2)
     own_part([2], 0)
-    w["q3"].s2()
-    kept["v"].d()
     own_part([2], 1)
     kept["k"].d()
-    kept["s"].b()
-    inside(pieces, 2)
-    kept["v"].e()
-    kept["s"].zs()
-    multiply("q3")
-    kept["k"].e()
-    low_part([2], 0)
     kept["s"].zf()
-    kept["s"].c()
-    low_part([0, 1], 1)
+    own_part([2], 2)
+    own_part([0, 1], 1)
+    kept["v"].d()
     kept["s"].d()
-    low_part([0, 1], 0)
     settle("q3")
     own_part([3], 0)
+    inside(pieces, 3)
+    kept["k"].e()
+    kept["s"].c()
+    own_part([3], 2)
+    kept["v"].e()
+    low_part([3], 0)
+    low_part([0, 1], 1)
+    low_part([2], 0)
+    low_part([0, 1], 0)
+    teacher(0)
+    kept["s"].near()
+    kept["s"].e()
+    own_part([3], 1)
+    incoming = arriving()
+    student(pieces, incoming, 3)
+    student(pieces, incoming, 2)
+    low_part([2], 1)
+    student(pieces, incoming, 1)
     low_part([3], 1)
-    low_part([3], 0)
-    own_part([3], 1)
-    kept["s"].e()
-    low_part([2], 1)
     teacher(2)
-    kept["s"].near()
-    incoming = arriving()
-    student(pieces, incoming, 1)
+    student(pieces, incoming, 0)
+    teacher(3)
     teacher(1)
-    inside(pieces, 3)
-    student(pieces, incoming, 3)
-    teacher(3)
-    student(pieces, incoming, 0)
-    teacher(0)
-    student(pieces, incoming, 2)
     for name in KINDS:
         w[name].sent()
         for cp in tiles(name):
@@ -634,20 +651,25 @@
     )
 
 
+def hand_over_kernel(teacher_ref, student_ref, teacher_out, student_out):
+    teacher_out[...] = teacher_ref[...]
+    student_out[...] = student_ref[...]
+
+
 def body(layer_input, attn_weight, rate_weight, rate_bias, decay_rate, skip_gain):
     vmem = pl.BlockSpec(memory_space=pltpu.VMEM)
     smem = pl.BlockSpec(memory_space=pltpu.SMEM)
     dma = pltpu.SemaphoreType.DMA
     near, base = tables()
     heads = (LOCAL_HEADS, TOK, HEAD_DIM)
-    return pl.pallas_call(
+    results = pl.pallas_call(
         window_kernel,
         name="window",
         out_shape=(
             jax.ShapeDtypeStruct((TOK, 512), BF),
             jax.ShapeDtypeStruct((TOK, 512), BF),
         ),
-        in_specs=[vmem] * 5 + [smem] * 3,
+        in_specs=[pl.BlockSpec(memory_space=pl.ANY)] + [vmem] * 4 + [smem] * 3,
         out_specs=(vmem, vmem),
         scratch_shapes=[
             pltpu.VMEM((2, 2, 8, 128, 256), BF),
@@ -681,14 +703,24 @@
             dma((3, COPIES)),
             dma,
             dma,
+            dma((16,)),
         ],
         compiler_params=pltpu.CompilerParams(
             collective_id=0, has_side_effects=True, vmem_limit_bytes=58 * 2**20
         ),
     )(
-        layer_input, attn_weight.reshape(128, 2560), rate_weight.T, jnp.asarray(near),
+        layer_input, attn_weight, rate_weight.T, jnp.asarray(near),
         jnp.asarray(base), rate_bias, decay_rate, skip_gain,
     )
+    half = pl.BlockSpec((TOK // 2, 512), lambda i: (i, 0))
+    return pl.pallas_call(
+        hand_over_kernel,
+        name="hand_over",
+        grid=(2,),
+        out_shape=(jax.ShapeDtypeStruct((TOK, 512), BF),) * 2,
+        in_specs=[half] * 2,
+        out_specs=(half,) * 2,
+    )(*results)
 
 
 def solution(mesh):

time: 99.3 us -> 93 us (0.937)
  local copies, waits for them, and re-layouts: 5.74 us -> 0 us
    unnamed x3 -> x0, local copies, waits for them, and re-layouts: 5.74 us -> none
    pallas_call x1, Pallas kernels: 92.2 us -> 89.9 us  [body(): pl.pallas_call(window_kernel, name='window', out_shape=(jax.ShapeDtypeStr...]
    pallas_call x0 -> x1, Pallas kernels: none -> 2.04 us  [body(): pl.pallas_call(hand_over_kernel, name='hand_over', grid=(2,), out_shape=(...]
where the time goes in v5:
time: 93 us; the launch traced here: 92.6 us
  Pallas kernels  92 us (99%)
    pallas_call x1, Pallas kernels, body(): pl.pallas_call(window_kernel, name='window', out_shape=(jax.ShapeDtypeStr...  89.9 us
    pallas_call x1, Pallas kernels, body(): pl.pallas_call(hand_over_kernel, name='hand_over', grid=(2,), out_shape=(...  2.04 us

profile of v5, /device:TPU:217, one launch (start us, length us, event | category | flops | bytes accessed | tf_op | source)
XLA Modules:
  0.0 92.6 jit_solution(3064714720945299662)
XLA Ops:
  0.6 89.9 %window.1 = (bf16[512,512]{1,0:T(8,128)(2,1)}, bf16[512,512]{1,0:T(8,128)(2,1)}) custom-call(bf16[512,2048]{1,0:T(8,128)(2,1)} %x_ref.1, bf16[128,2,1280]{2,1,0:T(2,128)(2,1)} %w_ref.1, bf16[16,2048]{1,0:T(8,128)(2,1)} %bitcast.1, f32[2,512,128]{2,1,0:T(8,128)} %constant.4.clone.near_ref, f32[2,16,128]{2,1,0:T(8,128)} %constant.5.clone.base_ref, f32[4]{0:T(128)} %bias_ref.1, ...), custom_call_target="tpu_custom_call" | custom-call | tf_op jit(solution)/shard_map/window/pallas_call | solution.py:665
  90.6 2.0 %hand_over.1 = (bf16[512,512]{1,0:T(8,128)(2,1)}, bf16[512,512]{1,0:T(8,128)(2,1)}) custom-call(bf16[512,512]{1,0:T(8,128)(2,1)} %get-tuple-element.4.teacher_ref, bf16[512,512]{1,0:T(8,128)(2,1)} %get-tuple-element.5.student_ref), custom_call_target="tpu_custom_call" | custom-call | tf_op jit(solution)/shard_map/hand_over/pallas_call | solution.py:716

commit v6 on v5

--- a/solution.py
+++ b/solution.py
@@ -485,23 +485,25 @@
             pl.when(c == 1)(lambda: absorb([(0, zy)], heads))
             return
 
-        def visit(j, carry):
-            absorb([(0, j), (1, j)], heads)
-            return carry
-
-        lax.fori_loop(zh * 4, zy, visit, 0)
+        if len(heads) > 1:
+
+            def visit(j, carry):
+                absorb([(0, j), (1, j)], heads)
+                return carry
+
+            lax.fori_loop(zh * 4, zy, visit, 0)
+            return
+        first, chips = zh * 4, p["y"]
+        pl.when(chips >= 2)(lambda: absorb([(k % 2, first + k // 2) for k in range(4)], heads))
+        last = zy - 1
+        pl.when(chips % 2 == 1)(lambda: absorb([(0, last), (1, last)], heads))
 
     def low_part(heads, part):
-        first = part * 2
-
-        def both():
-            if len(heads) > 1:
-                absorb([(0, first), (1, first)], heads)
-                absorb([(0, first + 1), (1, first + 1)], heads)
-            else:
-                absorb([(k % 2, first + k // 2) for k in range(4)], heads)
-
-        pl.when(zh == 1)(both)
+        if len(heads) > 1:
+            blocks = [(k % 2, part * 2 + k // 2) for k in range(4)]
+        else:
+            blocks = [(k % 2, k // 2) for k in range(8)]
+        pl.when(zh == 1)(lambda: absorb(blocks, heads))
 
     def teacher(h):
         done = acc[h]
@@ -610,9 +612,7 @@
     kept["s"].c()
     own_part([3], 2)
     kept["v"].e()
-    low_part([3], 0)
     low_part([0, 1], 1)
-    low_part([2], 0)
     low_part([0, 1], 0)
     teacher(0)
     kept["s"].near()

time: 93 us -> 92.3 us (level)
  no operation moved by 1% of the time
where the time goes in v6:
time: 92.3 us; the launch traced here: 91.9 us
  Pallas kernels  91.2 us (99%)
    pallas_call x1, Pallas kernels, body(): pl.pallas_call(window_kernel, name='window', out_shape=(jax.ShapeDtypeStr...  89.2 us
    pallas_call x1, Pallas kernels, body(): pl.pallas_call(hand_over_kernel, name='hand_over', grid=(2,), out_shape=(...  2.04 us

profile of v6, /device:TPU:217, one launch (start us, length us, event | category | flops | bytes accessed | tf_op | source)
XLA Modules:
  0.0 91.9 jit_solution(15942962816300450911)
XLA Ops:
  0.6 89.2 %window.1 = (bf16[512,512]{1,0:T(8,128)(2,1)}, bf16[512,512]{1,0:T(8,128)(2,1)}) custom-call(bf16[512,2048]{1,0:T(8,128)(2,1)} %x_ref.1, bf16[128,2,1280]{2,1,0:T(2,128)(2,1)} %w_ref.1, bf16[16,2048]{1,0:T(8,128)(2,1)} %bitcast.1, f32[2,512,128]{2,1,0:T(8,128)} %constant.4.clone.near_ref, f32[2,16,128]{2,1,0:T(8,128)} %constant.5.clone.base_ref, f32[4]{0:T(128)} %bias_ref.1, ...), custom_call_target="tpu_custom_call" | custom-call | tf_op jit(solution)/shard_map/window/pallas_call | solution.py:665
  89.8 2.0 %hand_over.1 = (bf16[512,512]{1,0:T(8,128)(2,1)}, bf16[512,512]{1,0:T(8,128)(2,1)}) custom-call(bf16[512,512]{1,0:T(8,128)(2,1)} %get-tuple-element.4.teacher_ref, bf16[512,512]{1,0:T(8,128)(2,1)} %get-tuple-element.5.student_ref), custom_call_target="tpu_custom_call" | custom-call | tf_op jit(solution)/shard_map/hand_over/pallas_call | solution.py:716

commit v7 on v6

--- a/solution.py
+++ b/solution.py
@@ -441,10 +441,15 @@
     def absorb(blocks, heads, diagonal=False):
         todo = [(b, h, i) for b in range(len(blocks)) for h in heads for i in range(TOK // HALF)]
 
+        def reach_of(i):
+            return (i + 1) * HALF if diagonal else TOK
+
         def scores(n):
             b, h, i = todo[n]
             keys = kall[(*blocks[b],)]
-            keys = jnp.concatenate([keys[:, k * 128 : k * 128 + 128] for k in range(4)], axis=0)
+            keys = jnp.concatenate(
+                [keys[:, k * 128 : k * 128 + 128] for k in range(reach_of(i) // 128)], axis=0
+            )
             out = dot_t(keys, rq[h, i * HALF : i * HALF + HALF])
             if diagonal:
                 at_u = lax.broadcasted_iota(jnp.int32, out.shape, 0)
@@ -473,7 +478,9 @@
                 top[h, 0:1, cols] = peak
             if ready is not None:
                 b, h, cols, weights, shrink = ready
-                mixed = dot(jnp.concatenate([vall[(*blocks[b],)], ones], axis=0), weights)
+                seen = weights.shape[0]
+                wide = jnp.concatenate([vall[(*blocks[b],)][:, :seen], ones[:, :seen]], axis=0)
+                mixed = dot(wide, weights)
                 acc[h, :, cols] = mixed if diagonal else mixed + acc[h, :, cols] * shrink
             ready = now
 

time: 92.3 us -> 92.3 us (level)
  no operation moved by 1% of the time
where the time goes in v7:
time: 92.3 us; the launch traced here: 91.8 us
  Pallas kernels  91.2 us (99%)
    pallas_call x1, Pallas kernels, body(): pl.pallas_call(window_kernel, name='window', out_shape=(jax.ShapeDtypeStr...  89.2 us
    pallas_call x1, Pallas kernels, body(): pl.pallas_call(hand_over_kernel, name='hand_over', grid=(2,), out_shape=(...  2.04 us

profile of v7, /device:TPU:217, one launch (start us, length us, event | category | flops | bytes accessed | tf_op | source)
XLA Modules:
  0.0 91.8 jit_solution(2838120879060044995)
XLA Ops:
  0.6 89.2 %window.1 = (bf16[512,512]{1,0:T(8,128)(2,1)}, bf16[512,512]{1,0:T(8,128)(2,1)}) custom-call(bf16[512,2048]{1,0:T(8,128)(2,1)} %x_ref.1, bf16[128,2,1280]{2,1,0:T(2,128)(2,1)} %w_ref.1, bf16[16,2048]{1,0:T(8,128)(2,1)} %bitcast.1, f32[2,512,128]{2,1,0:T(8,128)} %constant.4.clone.near_ref, f32[2,16,128]{2,1,0:T(8,128)} %constant.5.clone.base_ref, f32[4]{0:T(128)} %bias_ref.1, ...), custom_call_target="tpu_custom_call" | custom-call | tf_op jit(solution)/shard_map/window/pallas_call | solution.py:672
  89.8 2.0 %hand_over.1 = (bf16[512,512]{1,0:T(8,128)(2,1)}, bf16[512,512]{1,0:T(8,128)(2,1)}) custom-call(bf16[512,512]{1,0:T(8,128)(2,1)} %get-tuple-element.4.teacher_ref, bf16[512,512]{1,0:T(8,128)(2,1)} %get-tuple-element.5.student_ref), custom_call_target="tpu_custom_call" | custom-call | tf_op jit(solution)/shard_map/hand_over/pallas_call | solution.py:723
